TPU v7x, 512 devices: a whole 4x8x8 slice. The times are simulated.
512 devices in a mesh: comp: 64 (over z_lo, y, core), grp: 8 (over z_hi, x).
Axes of the slice: x: 4, y: 8, z: 8 (z_hi: 2, z_lo: 4; z = z_hi * 4 + z_lo), core: 2. Of those that a mesh axis runs over, the one named last changes fastest.
Arguments:
- spectrum: float32 [1152, 64, 1024], P('comp', 'grp'), may hold values from 0.1 to 1
- group_speed: float32 [2, 1152], replicated, may hold values from -0.25 to 0.25
- sea_mask: int32 [64, 1024], P('grp'), may hold values 0 or 1
- quad_index: int32 [4, 1152], replicated, may hold values from 0 to 1151
- coupling: bfloat16 [1152, 1152], replicated, may hold values from -0.1875 to 0.1875
- stokes_kernel: float32 [32, 1152], replicated, may hold values from -0.1875 to 0.1875
- ocean_flow: float32 [2, 16, 64, 1024], P(None, None, None, 'comp'), may hold values from -4 to 4
Outputs:
- forecast: float32 [1152, 64, 1024], P('comp', 'grp')
- ocean_state: float32 [2, 16, 64, 1024], P(None, None, None, 'comp')
All inputs are finite; a program needn't handle non-finite values. No bound on the sum of `sea_mask` on one device may be relied on, other than what follows from the above.
Results may differ from a plain program's by a relative error of at most 0.0004.
Values sent between devices are 32-bit elements; how exact they have to be, the bound alone decides.
No kernel may reach another device: no remote copies, remote signals or barrier semaphores. Data moves between devices by JAX's collectives and lax.ppermute only.
A program may use at most 64 MiB of HBM per device.

v0:
```python
import jax
import jax.numpy as jnp
from jax import lax
from jax.sharding import PartitionSpec as P

L = 16
STEPS = 2
SUB = 3


SOURCE_GAIN = 0.3
CURRENT_GAIN = 0.25
CORIOLIS = 0.3
VISCOSITY = 0.15
MIXING = 0.15


def extended(cells, sides, width):
    for axis, dim in sides:
        count = lax.axis_size(axis)
        ends = count - 1
        head = lax.slice_in_dim(cells, 0, width, axis=dim)
        tail = lax.slice_in_dim(cells, cells.shape[dim] - width, cells.shape[dim], axis=dim)
        cells = jnp.concatenate(
            [
                lax.ppermute(tail, axis, [(i, (i + 1) % count) for i in range(ends)]),
                cells,
                lax.ppermute(head, axis, [((i + 1) % count, i) for i in range(ends)]),
            ],
            axis=dim,
        )
    return cells


def upwind(padded, energy, speed_x, speed_y, wet_cells):
    westward = padded[:, 1:-1, :-2]
    eastward = padded[:, 1:-1, 2:]
    southward = padded[:, :-2, 1:-1]
    northward = padded[:, 2:, 1:-1]
    moved = (
        energy
        - jnp.maximum(speed_x, 0.0) * (energy - westward)
        - jnp.minimum(speed_x, 0.0) * (eastward - energy)
        - jnp.maximum(speed_y, 0.0) * (energy - southward)
        - jnp.minimum(speed_y, 0.0) * (northward - energy)
    )
    return moved * wet_cells


def wave_sources(points, quad_index, coupling, stokes_kernel, wet_flat):
    channels, rows_local, cols_local = points.shape
    columns = points.reshape(channels, rows_local * cols_local)
    for substep in range(SUB):
        first = jnp.take(columns, quad_index[0], axis=0)
        second = jnp.take(columns, quad_index[1], axis=0)
        third = jnp.take(columns, quad_index[2], axis=0)
        fourth = jnp.take(columns, quad_index[3], axis=0)
        interaction = (
            first * second * (third + fourth) - third * fourth * (first + second)
        ).astype(jnp.bfloat16)
        growth = jnp.dot(coupling, interaction, preferred_element_type=jnp.float32)
        columns = columns + wet_flat * (
            SOURCE_GAIN * growth / (1.0 + SOURCE_GAIN * jnp.abs(growth))
        )
    profile = jnp.dot(stokes_kernel, columns, precision=lax.Precision.HIGHEST)
    return (columns.reshape(points.shape), profile.reshape(2, L, rows_local, cols_local))


def laplace(padded, field):
    return (
        padded[:, 1:-1, 2:]
        + padded[:, 1:-1, :-2]
        + padded[:, 2:, 1:-1]
        + padded[:, :-2, 1:-1]
        - 4.0 * field
    )


def vertical(field):
    stacked = jnp.pad(field, ((1, 1), (0, 0), (0, 0)))
    return stacked[2:] + stacked[:-2] - 2.0 * field


def ocean_step(padded, flow, stokes):
    flow_x = flow[0]
    flow_y = flow[1]
    padded_x = padded[0]
    padded_y = padded[1]
    vortex = 0.5 * (padded_y[:, 1:-1, 2:] - padded_y[:, 1:-1, :-2]) - 0.5 * (
        padded_x[:, 2:, 1:-1] - padded_x[:, :-2, 1:-1]
    )
    drift_x = stokes[0]
    drift_y = stokes[1]
    new_x = (
        flow_x
        + CORIOLIS * (flow_y + drift_y)
        + vortex * drift_y
        + VISCOSITY * laplace(padded_x, flow_x)
        + MIXING * vertical(flow_x)
    )
    new_y = (
        flow_y
        - CORIOLIS * (flow_x + drift_x)
        - vortex * drift_x
        + VISCOSITY * laplace(padded_y, flow_y)
        + MIXING * vertical(flow_y)
    )
    return jnp.stack([new_x, new_y])


def local(spectrum, group_speed, sea_mask, quad_index, coupling, stokes_kernel, ocean_flow):
    rows_local = sea_mask.shape[0]
    cols_local = ocean_flow.shape[3]
    local_components = spectrum.shape[0]
    comp_place = lax.axis_index("comp")
    group_place = lax.axis_index("grp")
    wet_rows = (sea_mask == 1).astype(jnp.float32)
    wet_tile = lax.dynamic_slice_in_dim(wet_rows, comp_place * cols_local, cols_local, 1)
    wet_flat = wet_tile.reshape(1, rows_local * cols_local)
    own_speed = lax.dynamic_slice_in_dim(
        group_speed, comp_place * local_components, local_components, 1
    )
    flow = ocean_flow
    energy = spectrum
    for iteration in range(STEPS):
        top_level = lax.dynamic_slice_in_dim(flow[:, 0], group_place * rows_local, rows_local, 1)
        drift = lax.all_gather(CURRENT_GAIN * jnp.tanh(top_level), "comp", axis=2, tiled=True)
        padded = extended(energy, (("grp", 1),), 1)
        padded = jnp.pad(padded, ((0, 0), (0, 0), (1, 1)))
        speed_x = own_speed[0][:, None, None] + drift[0][None]
        speed_y = own_speed[1][:, None, None] + drift[1][None]
        energy = upwind(padded, energy, speed_x, speed_y, wet_rows[None])
        points, stokes = wave_sources(
            lax.all_to_all(energy, "comp", split_axis=2, concat_axis=0, tiled=True),
            quad_index,
            coupling,
            stokes_kernel,
            wet_flat,
        )
        energy = lax.all_to_all(points, "comp", split_axis=0, concat_axis=2, tiled=True)
        whole_stokes = lax.all_gather(stokes, "grp", axis=2, tiled=True)
        advance_padded = extended(flow, (("comp", 3),), 1)
        advance_padded = jnp.pad(advance_padded, ((0, 0), (0, 0), (1, 1), (0, 0)))
        result = ocean_step(advance_padded, flow, whole_stokes)
        flow = result
    return (energy, flow)


def solution(mesh):
    in_specs = (
        P("comp", "grp", None),
        P(),
        P("grp", None),
        P(),
        P(),
        P(),
        P(None, None, None, "comp"),
    )
    out_specs = (P("comp", "grp", None), P(None, None, None, "comp"))
    return jax.shard_map(local, mesh=mesh, in_specs=in_specs, out_specs=out_specs, check_vma=False)
```

profile of v0, /device:TPU:6, one launch (start us, length us, event | category | flops | bytes accessed | tf_op | source)
XLA Modules:
  0.0 645.1 jit_solution(14629305640031753987)
XLA Ops:
  2.8 11.0 %collective-permute-start = (f32[18,1,1024]{2,1,0:T(1,128)}, f32[18,1,1024]{2,1,0:T(1,128)}, u32[]{:S(2)}, u32[]{:S(2)}) collective-permute-start(f32[18,1,1024]{2,1,0:T(1,128)} %get-tuple-element.19), channel_id=1, source_target_pairs={{0,1},{1,2},{2,3},{3,4},{4,5},{5,6},{6,7},{8,9},{9,10},{10,11},{11... | collective-permute-start | bytes 221192 | tf_op jit(solution)/shard_map/ppermute | solution.py:26
  25.9 84.9 %all-gather = f32[2,1,8,1024]{2,0,1,3:T(2,128)S(1)} all-gather(f32[2,1,8,16]{2,0,1,3:T(2,128)S(1)} %fusion.108), channel_id=2, replica_groups=mesh['comp'=64,'grp'=8] {'comp'}, dimensions={3}, use_global_device_ids=true | all-gather | bytes 66560 | tf_op jit(solution)/shard_map/all_gather | solution.py:127
  121.6 3.7 copy.189
  125.3 6.2 reshape.326
  131.5 5.7 all-to-all-start
  141.4 14.9 %all-to-all-done = f32[64,1,2304]{2,1,0:T(1,128)} async-done(((f32[64,1,2304]{2,1,0:T(1,128)}), f32[64,1,2304]{2,1,0:T(1,128)}, u32[]{:S(2)}, u32[]{:S(2)}) %all-to-all-start) | async-done | bytes 589856 | tf_op jit(solution)/shard_map/all_to_all | solution.py:134
  156.9 3.2 reduce.8
  160.0 6.1 reshape.327
  166.1 6.6 %copy.191 = f32[64,18,8,16]{1,0,3,2:T(8,128)} copy(f32[64,18,8,16]{1,2,3,0:T(8,128)} %bitcast.150) | data formatting | bytes 1179648 | tf_op jit(solution)/shard_map/all_to_all | solution.py:134
  172.8 4.5 reshape.42
  178.6 3.1 gather_fusion.3
  181.7 3.3 gather_fusion.2
  185.1 3.1 gather_fusion.1
  188.2 3.3 gather_fusion
  191.5 5.0 bitcast_add_fusion.5
  197.8 3.1 gather_fusion.7
  200.9 3.3 gather_fusion.6
  204.2 3.1 gather_fusion.5
  207.3 3.3 gather_fusion.4
  210.7 5.0 bitcast_add_fusion.4
  217.0 3.1 gather_fusion.11
  220.1 3.3 gather_fusion.10
  223.4 3.1 gather_fusion.9
  226.5 3.7 gather_fusion.8
  230.2 4.2 bitcast_add_fusion.3
  237.5 4.6 reshape.328
  242.1 5.7 all-to-all-start.1
  250.9 59.4 %all_gather.13 = f32[2,16,64,16]{3,1,0,2:T(8,128)S(1)} all-gather(f32[2,16,8,16]{3,1,0,2:T(8,128)S(1)} %copy.209), channel_id=1, replica_groups=mesh['comp'=64,'grp'=8] {'grp'}, dimensions={2}, use_global_device_ids=true | all-gather | bytes 147456 | tf_op jit(solution)/shard_map/all_gather | solution.py:141
  317.4 84.6 %all-gather.1 = f32[2,1,8,1024]{2,0,1,3:T(2,128)} all-gather(f32[2,1,8,16]{2,0,1,3:T(2,128)S(1)} %fusion.107), channel_id=3, replica_groups=mesh['comp'=64,'grp'=8] {'comp'}, dimensions={3}, use_global_device_ids=true | all-gather | bytes 66560 | tf_op jit(solution)/shard_map/all_gather | solution.py:127
  402.0 4.0 reduce.9
  405.9 4.1 reshape.329
  410.0 6.0 copy.206
  416.0 5.0 all_to_all.54
  424.4 3.3 collective-permute-start.5
  427.8 3.4 fusion.116
  433.6 3.3 collective-permute-done.5
  439.3 3.7 copy.219
  443.0 6.2 reshape.330
  449.2 5.5 all-to-all-start.2
  461.3 13.0 %all-to-all-done.2 = f32[64,1,2304]{2,1,0:T(1,128)} async-done(((f32[64,1,2304]{2,1,0:T(1,128)}), f32[64,1,2304]{2,1,0:T(1,128)}, u32[]{:S(2)}, u32[]{:S(2)}) %all-to-all-start.2) | async-done | bytes 589856 | tf_op jit(solution)/shard_map/all_to_all | solution.py:134
  474.3 3.2 reduce.10
  477.4 6.3 reshape.331
  483.7 6.6 %copy.221 = f32[64,18,8,16]{1,0,3,2:T(8,128)} copy(f32[64,18,8,16]{1,2,3,0:T(8,128)} %bitcast.151) | data formatting | bytes 1179648 | tf_op jit(solution)/shard_map/all_to_all | solution.py:134
  490.4 4.5 reshape.45
  496.2 3.1 gather_fusion.15
  499.3 3.1 gather_fusion.14
  502.4 3.1 gather_fusion.13
  505.5 3.1 gather_fusion.12
  508.7 5.1 bitcast_add_fusion.2
  515.1 3.1 gather_fusion.19
  518.2 3.1 gather_fusion.18
  521.3 3.1 gather_fusion.17
  524.4 3.1 gather_fusion.16
  527.4 5.1 bitcast_add_fusion.1
  533.8 3.1 gather_fusion.23
  536.9 3.1 gather_fusion.22
  540.0 3.1 gather_fusion.21
  546.2 4.4 bitcast_add_fusion
  553.6 4.8 reshape.332
  558.4 6.6 %all-to-all-start.3 = ((f32[64,1,2304]{2,1,0:T(1,128)}), f32[64,1,2304]{2,1,0:T(1,128)}, u32[]{:S(2)}, u32[]{:S(2)}) async-start(f32[64,1,2304]{2,1,0:T(1,128)} %reshape.332), calls=%async_computation.3 | async-start | bytes 1179648 | tf_op jit(solution)/shard_map/all_to_all | solution.py:140
  568.3 53.8 %all_gather.15 = f32[2,16,64,16]{3,1,0,2:T(8,128)S(1)} all-gather(f32[2,16,8,16]{3,1,0,2:T(8,128)S(1)} %copy.237), channel_id=1, replica_groups=mesh['comp'=64,'grp'=8] {'grp'}, dimensions={2}, use_global_device_ids=true | all-gather | bytes 147456 | tf_op jit(solution)/shard_map/all_gather | solution.py:141
  626.9 3.2 reduce.11
  633.0 6.0 copy.236
  639.1 5.6 all_to_all.61
  (143 shorter events, 82.6 us)
Async XLA Ops:
  0.6 190.8 %copy-start = (bf16[1152,1152]{1,0:T(8,128)(2,1)S(1)}, bf16[1152,1152]{1,0:T(8,128)(2,1)}, u32[]{:S(2)}) copy-start(bf16[1152,1152]{1,0:T(8,128)(2,1)} %param.13) | copy-start | bytes 7962628
  2.8 114.6 %copy-start.7 = (f32[18,8,1024]{2,1,0:T(8,128)S(1)}, f32[18,8,1024]{2,1,0:T(8,128)}, u32[]{:S(2)}) copy-start(f32[18,8,1024]{2,1,0:T(8,128)} %param.9) | copy-start | bytes 1769476
  2.8 114.6 %collective-permute-start = (f32[18,1,1024]{2,1,0:T(1,128)}, f32[18,1,1024]{2,1,0:T(1,128)}, u32[]{:S(2)}, u32[]{:S(2)}) collective-permute-start(f32[18,1,1024]{2,1,0:T(1,128)} %get-tuple-element.19), channel_id=1, source_target_pairs={{0,1},{1,2},{2,3},{3,4},{4,5},{5,6},{6,7},{8,9},{9,10},{10,11},{11... | collective-permute-start | bytes 221192 | tf_op jit(solution)/shard_map/ppermute | solution.py:26
  13.8 103.7 %collective-permute-start.1 = (f32[18,1,1024]{2,1,0:T(1,128)}, f32[18,1,1024]{2,1,0:T(1,128)}, u32[]{:S(2)}, u32[]{:S(2)}) collective-permute-start(f32[18,1,1024]{2,1,0:T(1,128)} %get-tuple-element.20), channel_id=1, source_target_pairs={{1,0},{2,1},{3,2},{4,3},{5,4},{6,5},{7,6},{9,8},{10,9},{11,10},{12... | collective-permute-start | bytes 221192 | tf_op jit(solution)/shard_map/ppermute | solution.py:28
  16.7 123.8 %copy-start.1 = (f32[2,16,64,16]{2,1,3,0:T(8,128)}, f32[2,16,64,16]{2,1,3,0:T(8,128)S(1)}, u32[]{:S(2)}) copy-start(f32[2,16,64,16]{2,1,3,0:T(8,128)S(1)} %copy.207) | copy-start | bytes 393220
  17.4 123.1 %collective-permute-start.2 = (f32[2,16,64,1]{2,1,3,0:T(8,128)}, f32[2,16,64,1]{2,1,3,0:T(8,128)}, u32[]{:S(2)}, u32[]{:S(2)}) collective-permute-start(f32[2,16,64,1]{2,1,3,0:T(8,128)} %get-tuple-element.31), channel_id=1, source_target_pairs={{0,8},{8,16},{16,24},{24,32},{32,40},{40,48},{48,56},{56,64},{64,7... | collective-permute-start | bytes 24584 | tf_op jit(solution)/shard_map/ppermute | solution.py:26
  19.5 121.1 %collective-permute-start.3 = (f32[2,16,64,1]{2,1,3,0:T(8,128)}, f32[2,16,64,1]{2,1,3,0:T(8,128)}, u32[]{:S(2)}, u32[]{:S(2)}) collective-permute-start(f32[2,16,64,1]{2,1,3,0:T(8,128)} %get-tuple-element.32), channel_id=1, source_target_pairs={{8,0},{16,8},{24,16},{32,24},{40,32},{48,40},{56,48},{64,56},{72,6... | collective-permute-start | bytes 24584 | tf_op jit(solution)/shard_map/ppermute | solution.py:28
  23.7 116.1 %copy-start.11 = (f32[8,1024]{1,0:T(8,128)}, f32[8,1024]{1,0:T(8,128)S(1)}, u32[]{:S(2)}) copy-start(f32[8,1024]{1,0:T(8,128)S(1)} %compare_convert_fusion) | copy-start | bytes 98308
  24.6 1.2 copy-start.13
  24.6 1.2 copy-start.15
  24.6 1.2 copy-start.17
  24.6 1.2 copy-start.19
  125.3 11.9 %copy-start.21 = (s32[1152]{0:T(1024)S(1)}, s32[1152]{0:T(1024)}, u32[]{:S(2)}) copy-start(s32[1152]{0:T(1024)} %get-tuple-element.38) | copy-start | bytes 13828
  125.3 12.5 %copy-start.18 = (s32[1152]{0:T(1024)S(1)}, s32[1152]{0:T(1024)}, u32[]{:S(2)}) copy-start(s32[1152]{0:T(1024)} %copy-done.17) | copy-start | bytes 13828
  125.3 12.5 %copy-start.20 = (s32[1152]{0:T(1024)S(1)}, s32[1152]{0:T(1024)}, u32[]{:S(2)}) copy-start(s32[1152]{0:T(1024)} %copy-done.19) | copy-start | bytes 13828
  125.3 13.1 %copy-start.14 = (s32[1152]{0:T(1024)S(1)}, s32[1152]{0:T(1024)}, u32[]{:S(2)}) copy-start(s32[1152]{0:T(1024)} %copy-done.13) | copy-start | bytes 13828
  125.3 13.1 %copy-start.16 = (s32[1152]{0:T(1024)S(1)}, s32[1152]{0:T(1024)}, u32[]{:S(2)}) copy-start(s32[1152]{0:T(1024)} %copy-done.15) | copy-start | bytes 13828
  131.5 24.7 %all-to-all-start = ((f32[64,1,2304]{2,1,0:T(1,128)}), f32[64,1,2304]{2,1,0:T(1,128)}, u32[]{:S(2)}, u32[]{:S(2)}) async-start(f32[64,1,2304]{2,1,0:T(1,128)} %reshape.326), calls=%async_computation | async-start | bytes 1179648 | tf_op jit(solution)/shard_map/all_to_all | solution.py:134
  242.1 159.9 %all-to-all-start.1 = ((f32[64,1,2304]{2,1,0:T(1,128)}), f32[64,1,2304]{2,1,0:T(1,128)}, u32[]{:S(2)}, u32[]{:S(2)}) async-start(f32[64,1,2304]{2,1,0:T(1,128)} %reshape.328), calls=%async_computation.1 | async-start | bytes 1179648 | tf_op jit(solution)/shard_map/all_to_all | solution.py:140
  250.0 64.6 %copy-start.2 = (f32[2,16,64,16]{2,1,3,0:T(8,128)S(1)}, f32[2,16,64,16]{2,1,3,0:T(8,128)}, u32[]{:S(2)}) copy-start(f32[2,16,64,16]{2,1,3,0:T(8,128)} %copy-done.1) | copy-start | bytes 393220
  315.9 94.1 %copy-start.3 = (f32[16,64,16]{1,0,2:T(8,128)}, f32[16,64,16]{1,0,2:T(8,128)S(1)}, u32[]{:S(2)}) copy-start(f32[16,64,16]{1,0,2:T(8,128)S(1)} %fusion.63) | copy-start | bytes 196612
  317.2 92.8 %copy-start.5 = (f32[16,64,16]{1,0,2:T(8,128)}, f32[16,64,16]{1,0,2:T(8,128)S(1)}, u32[]{:S(2)}) copy-start(f32[16,64,16]{1,0,2:T(8,128)S(1)} %fusion.67) | copy-start | bytes 196612
  421.8 15.9 %copy-start.12 = (f32[8,1024]{1,0:T(8,128)S(1)}, f32[8,1024]{1,0:T(8,128)}, u32[]{:S(2)}) copy-start(f32[8,1024]{1,0:T(8,128)} %copy-done.11) | copy-start | bytes 98308
  421.8 15.9 %copy-start.22 = (f32[18]{0:T(128)S(1)}, f32[18]{0:T(128)}, u32[]{:S(2)}) copy-start(f32[18]{0:T(128)} %get-tuple-element.33) | copy-start | bytes 220
  421.8 15.9 %copy-start.23 = (f32[18]{0:T(128)S(1)}, f32[18]{0:T(128)}, u32[]{:S(2)}) copy-start(f32[18]{0:T(128)} %get-tuple-element.34) | copy-start | bytes 220
  421.8 11.8 %collective-permute-start.4 = (f32[18,1,1024]{2,1,0:T(1,128)}, f32[18,1,1024]{2,1,0:T(1,128)S(1)}, u32[]{:S(2)}, u32[]{:S(2)}) collective-permute-start(f32[18,1,1024]{2,1,0:T(1,128)} %get-tuple-element.17), channel_id=1, source_target_pairs={{0,1},{1,2},{2,3},{3,4},{4,5},{5,6},{6,7},{8,9},{9,10},{10,11},{11... | collective-permute-start | bytes 221192 | tf_op jit(solution)/shard_map/ppermute | solution.py:26
  424.4 12.5 %collective-permute-start.5 = (f32[18,1,1024]{2,1,0:T(1,128)}, f32[18,1,1024]{2,1,0:T(1,128)S(1)}, u32[]{:S(2)}, u32[]{:S(2)}) collective-permute-start(f32[18,1,1024]{2,1,0:T(1,128)} %get-tuple-element.18), channel_id=1, source_target_pairs={{1,0},{2,1},{3,2},{4,3},{5,4},{6,5},{7,6},{9,8},{10,9},{11,10},{12... | collective-permute-start | bytes 221192 | tf_op jit(solution)/shard_map/ppermute | solution.py:28
  443.0 11.7 %copy-start.4 = (f32[16,64,16]{1,0,2:T(8,128)S(1)}, f32[16,64,16]{1,0,2:T(8,128)}, u32[]{:S(2)}) copy-start(f32[16,64,16]{1,0,2:T(8,128)} %copy-done.3) | copy-start | bytes 196612
  443.0 11.7 %copy-start.6 = (f32[16,64,16]{1,0,2:T(8,128)S(1)}, f32[16,64,16]{1,0,2:T(8,128)}, u32[]{:S(2)}) copy-start(f32[16,64,16]{1,0,2:T(8,128)} %copy-done.5) | copy-start | bytes 196612
  449.2 25.1 %all-to-all-start.2 = ((f32[64,1,2304]{2,1,0:T(1,128)}), f32[64,1,2304]{2,1,0:T(1,128)}, u32[]{:S(2)}, u32[]{:S(2)}) async-start(f32[64,1,2304]{2,1,0:T(1,128)} %reshape.330), calls=%async_computation.2 | async-start | bytes 1179648 | tf_op jit(solution)/shard_map/all_to_all | solution.py:134
  454.7 4.4 collective-permute-start.7
  456.0 3.9 collective-permute-start.6
  496.2 3.1 copy-start.9
  502.4 3.1 copy-start.10
  505.5 3.1 copy-start.24
  505.5 3.1 copy-start.25
  505.5 3.1 copy-start.26
  505.5 3.1 copy-start.27
  543.1 3.1 copy-start.28
  550.6 3.0 copy-start.8
  558.4 68.5 %all-to-all-start.3 = ((f32[64,1,2304]{2,1,0:T(1,128)}), f32[64,1,2304]{2,1,0:T(1,128)}, u32[]{:S(2)}, u32[]{:S(2)}) async-start(f32[64,1,2304]{2,1,0:T(1,128)} %reshape.332), calls=%async_computation.3 | async-start | bytes 1179648 | tf_op jit(solution)/shard_map/all_to_all | solution.py:140
where the time goes:
time: 654 us; the launch traced here: 645 us
  blocking collectives  283 us (43%)
  local copies, waits for them, and re-layouts  215 us (33%)
  starting transfers between devices  49.9 us (8%)
  matrix products  32.8 us (5%)
  waiting for transfers between devices  31.9 us (5%)
  other arithmetic  31.1 us (5%)
    all_gather x2, blocking collectives, local(): lax.all_gather(CURRENT_GAIN * jnp.tanh(top_level), 'comp', axis=2, tiled=...  169 us
    all_gather x2, blocking collectives, local(): whole_stokes = lax.all_gather(stokes, 'grp', axis=2, tiled=True)  113 us
    unnamed x71, local copies, waits for them, and re-layouts  48.3 us
    dot_general x6, matrix products, wave_sources(): growth = jnp.dot(coupling, interaction, preferred_element_type=jnp.float32)  28.9 us
    all_to_all x2, waiting for transfers between devices, local(): lax.all_to_all(energy, 'comp', split_axis=2, concat_axis=0, tiled=True)  27.8 us
    all_to_all x4, local copies, waits for them, and re-layouts, local(): lax.all_to_all(points, 'comp', split_axis=0, concat_axis=2, tiled=True)  22.6 us
    gather x6, local copies, waits for them, and re-layouts, wave_sources(): first = jnp.take(columns, quad_index[0], axis=0)  19.6 us
    gather x6, local copies, waits for them, and re-layouts, wave_sources(): third = jnp.take(columns, quad_index[2], axis=0)  19.2 us
  transfers between devices with their start and end apart: 12, of which 4 were waited for; matrix products, arithmetic and copies ran while one was open for 9% of the time, Pallas kernels for 0%

commit v1 on v0

v1 whole, which is shorter than its diff:
```python
import functools

import jax
import jax.numpy as jnp
from jax import lax
from jax.experimental import pallas as pl
from jax.experimental.pallas import tpu as pltpu
from jax.sharding import PartitionSpec as P

L = 16
STEPS = 2
SUB = 3

SOURCE_GAIN = 0.3
CURRENT_GAIN = 0.25
CORIOLIS = 0.3
VISCOSITY = 0.15
MIXING = 0.15

ROWS = 8
COLS = 16
LANES = 128
FIELDS = 2 * L

VMEM = pl.BlockSpec(memory_space=pltpu.VMEM)
SMEM = pl.BlockSpec(memory_space=pltpu.SMEM)
SMALL = pltpu.CompilerParams(vmem_limit_bytes=16 * 2**20)


def roll(x, shift, axis=1):
    shift %= x.shape[axis]
    return pltpu.roll(x, shift, axis) if shift else x


def lane_places():
    lane = lax.broadcasted_iota(jnp.int32, (8, LANES), 1)
    return lane // COLS, lane % COLS


def exchange_blocks(x):
    sub = lax.broadcasted_iota(jnp.int32, (8, LANES), 0)
    block, _ = lane_places()
    for bit in (1, 2, 4):
        in_sub = (sub & bit) != 0
        in_block = (block & bit) != 0
        up = roll(roll(x, -bit, 0), bit * COLS)
        down = roll(roll(x, bit, 0), -bit * COLS)
        x = jnp.where(in_sub == in_block, x, jnp.where(in_block, up, down))
    return x


def to_points_kernel(x_ref, o_ref):
    parts = x_ref.shape[0]

    def one(k, carry):
        for j in range(x_ref.shape[2] // LANES):
            tile = exchange_blocks(x_ref[k, :, j * LANES : (j + 1) * LANES])
            o_ref[pl.ds(j * 8 * parts + k, 8, stride=parts), :] = tile
        return carry

    lax.fori_loop(0, parts, one, 0)


def from_points_kernel(x_ref, o_ref):
    parts = o_ref.shape[0]

    def one(k, carry):
        for j in range(o_ref.shape[2] // LANES):
            tile = x_ref[pl.ds(j * 8 * parts + k, 8, stride=parts), :]
            o_ref[k, :, j * LANES : (j + 1) * LANES] = exchange_blocks(tile)
        return carry

    lax.fori_loop(0, parts, one, 0)


def tile_rows(start, count=8):
    return pl.ds(start if isinstance(start, int) else pl.multiple_of(start, 8), count)


def pack_group(load, count, m, up_ref, down_ref, east_ref, west_ref):
    block, col = lane_places()
    east = west = None
    for h in range((count + 7) // 8):
        up = down = None
        for i in range(min(8, count - 8 * h)):
            n = 8 * h + i
            tile = load(n)
            u = roll(tile, (i - (ROWS - 1)) * COLS)
            d = roll(tile, i * COLS)
            e = roll(tile, n - (COLS - 1))
            w = roll(tile, n)
            up = u if up is None else jnp.where(block == i, u, up)
            down = d if down is None else jnp.where(block == i, d, down)
            east = e if east is None else jnp.where(col == n, e, east)
            west = w if west is None else jnp.where(col == n, w, west)
        up_ref[tile_rows((2 * m + h) * 8), :] = up
        down_ref[tile_rows((2 * m + h) * 8), :] = down
    east_ref[tile_rows(m * 8), :] = east
    west_ref[tile_rows(m * 8), :] = west


def pack_all(e_ref, f_ref, channels, edges):
    def one(m, carry):
        pack_group(lambda n: e_ref[tile_rows(m * 128 + n * 8), :], 16, m, *edges)
        return carry

    lax.fori_loop(0, channels // 128, one, 0)
    pack_group(lambda n: f_ref[n * 8 : n * 8 + 8, :], FIELDS // 8, channels // 128, *edges)


def neighbours(tile, n, m, south_ref, north_ref, west_ref, east_ref):
    block, col = lane_places()
    h, i = divmod(n, 8)
    south = roll(south_ref[tile_rows((2 * m + h) * 8), :], -i * COLS)
    north = roll(north_ref[tile_rows((2 * m + h) * 8), :], (ROWS - 1 - i) * COLS)
    west = roll(west_ref[tile_rows(m * 8), :], -n)
    east = roll(east_ref[tile_rows(m * 8), :], COLS - 1 - n)
    return (
        jnp.where(col == 0, west, roll(tile, 1)),
        jnp.where(col == COLS - 1, east, roll(tile, -1)),
        jnp.where(block == 0, south, roll(tile, COLS)),
        jnp.where(block == ROWS - 1, north, roll(tile, -COLS)),
    )


def edges_kernel(e_ref, f_ref, *edges):
    pack_all(e_ref, f_ref, e_ref.shape[0], edges)


def step_kernel(
    last,
    index_ref,
    e_in_ref,
    f_in_ref,
    wet_ref,
    speed_ref,
    coupling_ref,
    profile_ref,
    south_ref,
    north_ref,
    west_ref,
    east_ref,
    e_out_ref,
    f_out_ref,
    *rest,
):
    edges, (e_ref, inter_ref) = rest[:-2], rest[-2:]
    channels = e_in_ref.shape[0]
    quads = inter_ref.shape[0]
    halos = (south_ref, north_ref, west_ref, east_ref)
    wet = jnp.broadcast_to(wet_ref[...], (8, LANES))
    drift_x = jnp.broadcast_to(CURRENT_GAIN * jnp.tanh(f_in_ref[0:1, :]), (8, LANES))
    drift_y = jnp.broadcast_to(CURRENT_GAIN * jnp.tanh(f_in_ref[L : L + 1, :]), (8, LANES))

    def advect(m, carry):
        for n in range(16):
            rows = tile_rows(m * 128 + n * 8)
            tile = e_in_ref[rows, :]
            speed = speed_ref[rows, :]
            a_x = speed[:, 0:1] + drift_x
            a_y = speed[:, 1:2] + drift_y
            west, east, south, north = neighbours(tile, n, m, *halos)
            moved = (
                tile
                - jnp.maximum(a_x, 0.0) * (tile - west)
                - jnp.minimum(a_x, 0.0) * (east - tile)
                - jnp.maximum(a_y, 0.0) * (tile - south)
                - jnp.minimum(a_y, 0.0) * (north - tile)
            )
            e_ref[rows, :] = moved * wet
        return carry

    lax.fori_loop(0, channels // 128, advect, 0)

    sub = lax.broadcasted_iota(jnp.int32, (8, LANES), 0)
    here = [sub == s for s in range(8)]

    def gathered(base):
        picked = []
        for j in range(4):
            rows = None
            for s in range(8):
                row = e_ref[pl.ds(index_ref[base + j * 8 + s], 8, stride=0), :]
                rows = row if rows is None else jnp.where(here[s], row, rows)
            picked.append(rows)
        first, second, third, fourth = picked
        return first * second * (third + fourth) - third * fourth * (first + second)

    def interactions(i, carry):
        for t in range(2):
            base = i * 128 + t * 64
            both = jnp.concatenate([gathered(base), gathered(base + 32)], axis=0)
            inter_ref[pl.ds(pl.multiple_of(i * 32 + t * 16, 16), 16), :] = both.astype(jnp.bfloat16)
        return carry

    def substep(_, carry):
        lax.fori_loop(0, quads // 32, interactions, 0)
        growth = jnp.dot(coupling_ref[...], inter_ref[...], preferred_element_type=jnp.float32)
        gained = SOURCE_GAIN * growth / (1.0 + SOURCE_GAIN * jnp.abs(growth))
        e_ref[0:channels, :] = e_ref[0:channels, :] + wet_ref[...] * gained
        return carry

    lax.fori_loop(0, SUB, substep, 0)

    energy = e_ref[0:channels, :]
    e_out_ref[...] = energy
    stokes = jnp.dot(
        profile_ref[...], energy, precision=lax.Precision.HIGHEST, preferred_element_type=jnp.float32
    )

    tiles = [f_in_ref[n * 8 : n * 8 + 8, :] for n in range(FIELDS // 8)]
    around = [neighbours(tile, n, channels // 128, *halos) for n, tile in enumerate(tiles)]
    half = L // 8
    level = lax.broadcasted_iota(jnp.int32, (L, LANES), 0)

    def field(lo):
        whole = jnp.concatenate(tiles[lo : lo + half], axis=0)
        sides = [jnp.concatenate([around[n][d] for n in range(lo, lo + half)], axis=0) for d in range(4)]
        above = jnp.where(level == 0, 0.0, roll(whole, 1, 0))
        below = jnp.where(level == L - 1, 0.0, roll(whole, -1, 0))
        mixed = VISCOSITY * (sides[1] + sides[0] + sides[3] + sides[2] - 4.0 * whole) + MIXING * (
            below + above - 2.0 * whole
        )
        return whole, sides, mixed

    flow_x, sides_x, mixed_x = field(0)
    flow_y, sides_y, mixed_y = field(half)
    vortex = 0.5 * (sides_y[1] - sides_y[0]) - 0.5 * (sides_x[3] - sides_x[2])
    stokes_x = stokes[0:L]
    stokes_y = stokes[L : 2 * L]
    f_out_ref[0:L, :] = flow_x + CORIOLIS * (flow_y + stokes_y) + vortex * stokes_y + mixed_x
    f_out_ref[L : 2 * L, :] = flow_y - CORIOLIS * (flow_x + stokes_x) - vortex * stokes_x + mixed_y

    if not last:
        pack_all(e_ref, f_out_ref, channels, edges)


def exchange(values, axis):
    rows, lanes = values.shape
    moved = lax.all_to_all(values.reshape(rows, 1, lanes), axis, split_axis=0, concat_axis=0, tiled=True)
    return moved.reshape(rows, lanes)


def send_edges(edges):
    up, down, east, west = edges

    def shift(value, axis, by):
        count = lax.axis_size(axis)
        pairs = [(i, i + by) for i in range(count) if 0 <= i + by < count]
        return lax.ppermute(value, axis, pairs)

    south = shift(up, "grp", 1)
    north = shift(down, "grp", -1)
    from_west = shift(east, "comp", 1)
    from_east = shift(west, "comp", -1)
    return south, north, from_west, from_east


def local(spectrum, group_speed, sea_mask, quad_index, coupling, stokes_kernel, ocean_flow):
    parts, rows_local, columns = spectrum.shape
    cols_local = ocean_flow.shape[3]
    peers = columns // cols_local
    groups = ocean_flow.shape[2] // rows_local
    channels = parts * peers
    quads = quad_index.shape[1]
    comp_place = lax.axis_index("comp")
    group_place = lax.axis_index("grp")

    float_of = lambda *shape: jax.ShapeDtypeStruct(shape, jnp.float32)
    edge_shapes = [float_of((channels // 64 + 1) * 8, LANES)] * 2 + [
        float_of((channels // 128 + 1) * 8, LANES)
    ] * 2

    wet_rows = (sea_mask == 1).astype(jnp.float32)
    wet = lax.dynamic_slice_in_dim(wet_rows, comp_place * cols_local, cols_local, 1).reshape(1, LANES)
    flow = lax.dynamic_slice_in_dim(ocean_flow, group_place * rows_local, rows_local, 2).reshape(FIELDS, LANES)
    index = quad_index.reshape(4, quads // 8, 8).transpose(1, 0, 2).reshape(4 * quads)
    speed = group_speed.T

    sent = pl.pallas_call(
        to_points_kernel, out_shape=float_of(channels, LANES), in_specs=[VMEM], out_specs=VMEM, compiler_params=SMALL, name="to_points"
    )(spectrum)
    energy = exchange(sent, "comp")
    edges = pl.pallas_call(
        edges_kernel, out_shape=edge_shapes, in_specs=[VMEM] * 2, out_specs=[VMEM] * 4, compiler_params=SMALL, name="edges"
    )(energy, flow)
    for iteration in range(STEPS):
        last = iteration == STEPS - 1
        halos = send_edges(edges)
        outs = [float_of(channels, LANES), float_of(FIELDS, LANES)] + ([] if last else edge_shapes)
        energy, flow, *edges = pl.pallas_call(
            functools.partial(step_kernel, last),
            out_shape=outs,
            in_specs=[SMEM] + [VMEM] * 10,
            out_specs=[VMEM] * len(outs),
            scratch_shapes=[pltpu.VMEM((channels + 8, LANES), jnp.float32), pltpu.VMEM((quads, LANES), jnp.bfloat16)],
            compiler_params=SMALL,
            name="last_step" if last else "step",
        )(index, energy, flow, wet, speed, coupling, stokes_kernel, *halos)
    returned = exchange(energy, "comp")
    forecast = pl.pallas_call(
        from_points_kernel,
        out_shape=float_of(parts, rows_local, columns),
        in_specs=[VMEM],
        out_specs=VMEM,
        compiler_params=SMALL,
        name="from_points",
    )(returned)
    copies = jnp.broadcast_to(flow[None], (groups, FIELDS, LANES)).reshape(groups * FIELDS, LANES)
    rows = exchange(copies, "grp").reshape(groups, 2, L, rows_local, cols_local)
    ocean = rows.transpose(1, 2, 0, 3, 4).reshape(2, L, groups * rows_local, cols_local)
    return forecast, ocean


def solution(mesh):
    in_specs = (
        P("comp", "grp", None),
        P(),
        P("grp", None),
        P(),
        P(),
        P(),
        P(None, None, None, "comp"),
    )
    out_specs = (P("comp", "grp", None), P(None, None, None, "comp"))
    return jax.shard_map(local, mesh=mesh, in_specs=in_specs, out_specs=out_specs, check_vma=False)
```

time: 654 us -> 187 us (0.29)
  blocking collectives: 283 us -> 14.9 us
  local copies, waits for them, and re-layouts: 215 us -> 15.2 us
  Pallas kernels: 0 us -> 56.8 us
  matrix products: 32.8 us -> 0 us
  other arithmetic: 31.1 us -> 1.71 us
  waiting for transfers between devices: 31.9 us -> 43.3 us
    all_gather x4 -> x0, blocking collectives: 283 us -> none  [the longest x2 169 us: local(): lax.all_gather(CURRENT_GAIN * jnp.tanh(top_level), 'comp', axis=2, tiled=...]
    gather x24 -> x0, local copies, waits for them, and re-layouts: 76 us -> none  [the longest x6 19.6 us: wave_sources(): first = jnp.take(columns, quad_index[0], axis=0)]
    pallas_call x0 -> x5, Pallas kernels: none -> 56.8 us  [the longest x2 46 us: local(): pl.pallas_call(functools.partial(step_kernel, last), out_shape=outs, in_s...]
    unnamed x71 -> x18, local copies, waits for them, and re-layouts: 48.3 us -> 6.71 us
    all_to_all x7 -> x1, local copies, waits for them, and re-layouts: 36.5 us -> 0.51 us  [exchange(): lax.all_to_all(values.reshape(rows, 1, lanes), axis, split_axis=0, concat...]
    dot_general x8 -> x0, matrix products: 32.8 us -> none  [the longest x6 28.9 us: wave_sources(): growth = jnp.dot(coupling, interaction, preferred_element_type=jnp.float32)]
    reshape x10 -> x5, local copies, waits for them, and re-layouts: 18.7 us -> 3.33 us  [the longest x2 2.14 us: local(): quad_index.reshape(4, quads // 8, 8).transpose(1, 0, 2).reshape(4 * quads)]
    all_to_all x0 -> x1, blocking collectives: none -> 14.9 us  [exchange(): lax.all_to_all(values.reshape(rows, 1, lanes), axis, split_axis=0, concat...]
  transfers between devices with their start and end apart: 12 -> 10, of which waited for: 4 -> 5; matrix products, arithmetic and copies ran while one was open for 9% -> 7% of each run, Pallas kernels for 0% -> 0%
where the time goes in v1:
time: 187 us; the launch traced here: 183 us
  Pallas kernels  56.8 us (30%)
  starting transfers between devices  50.6 us (27%)
  waiting for transfers between devices  43.3 us (23%)
  local copies, waits for them, and re-layouts  15.2 us (8%)
  blocking collectives  14.9 us (8%)
    pallas_call x2, Pallas kernels, local(): pl.pallas_call(functools.partial(step_kernel, last), out_shape=outs, in_s...  46 us
    all_to_all x2, waiting for transfers between devices, exchange(): lax.all_to_all(values.reshape(rows, 1, lanes), axis, split_axis=0, concat...  31.8 us
    all_to_all x2, starting transfers between devices, exchange(): lax.all_to_all(values.reshape(rows, 1, lanes), axis, split_axis=0, concat...  25.3 us
    ppermute x8, starting transfers between devices, shift(): return lax.ppermute(value, axis, pairs)  25.3 us
    all_to_all x1, blocking collectives, exchange(): lax.all_to_all(values.reshape(rows, 1, lanes), axis, split_axis=0, concat...  14.9 us
    ppermute x8, waiting for transfers between devices, shift(): return lax.ppermute(value, axis, pairs)  11.5 us
    unnamed x18, local copies, waits for them, and re-layouts  6.71 us
    pallas_call x1, Pallas kernels, local(): pl.pallas_call(from_points_kernel, out_shape=float_of(parts, rows_local,...  4.89 us
  transfers between devices with their start and end apart: 10, of which 5 were waited for; matrix products, arithmetic and copies ran while one was open for 7% of the time, Pallas kernels for 0%

profile of v1, /device:TPU:6, one launch (start us, length us, event | category | flops | bytes accessed | tf_op | source)
XLA Modules:
  0.0 183.3 jit_solution(14487310029828692544)
XLA Ops:
  0.6 0.0 copy-start
  0.6 0.0 copy-start.5
  0.7 1.1 copy-done.5
  1.8 0.0 copy-start.7
  1.8 4.1 %to_points.1 = f32[1152,128]{1,0:T(8,128)S(1)} custom-call(f32[18,8,1024]{2,1,0:T(8,128)S(1)} %copy-done.5), custom_call_target="tpu_custom_call" | custom-call | tf_op jit(solution)/shard_map/to_points/pallas_call | solution.py:280
  5.8 0.0 copy-start.4
  5.9 0.8 copy-done.4
  6.7 0.0 copy-start.1
  6.7 13.8 %all-to-all-start = ((f32[1152,1,128]{2,1,0:T(1,128)}), f32[1152,1,128]{2,1,0:T(1,128)S(1)}, u32[]{:S(2)}, u32[]{:S(2)}) async-start(f32[1152,1,128]{2,1,0:T(1,128)} %bitcast.22), calls=%async_computation | async-start | bytes 1179648 | tf_op jit(solution)/shard_map/all_to_all | solution.py:240
  20.5 0.0 copy-done
  20.5 0.8 constant_dynamic-slice_fusion
  21.3 1.7 copy.18
  23.1 1.0 reshape.36.f_ref.f_in_ref
  24.1 15.6 %all-to-all-done = f32[1152,1,128]{2,1,0:T(1,128)S(1)} async-done(((f32[1152,1,128]{2,1,0:T(1,128)}), f32[1152,1,128]{2,1,0:T(1,128)S(1)}, u32[]{:S(2)}, u32[]{:S(2)}) %all-to-all-start) | async-done | bytes 589856 | tf_op jit(solution)/shard_map/all_to_all | solution.py:240
  39.6 1.9 %edges.1 = (f32[152,128]{1,0:T(8,128)}, f32[152,128]{1,0:T(8,128)}, f32[80,128]{1,0:T(8,128)}, f32[80,128]{1,0:T(8,128)}) custom-call(f32[1152,128]{1,0:T(8,128)S(1)} %bitcast.18, f32[32,128]{1,0:T(8,128)S(1)} %reshape.36.f_ref.f_in_ref), custom_call_target="tpu_custom_call" | custom-call | tf_op jit(solution)/shard_map/edges/pallas_call | solution.py:284
  41.5 2.4 %collective-permute-start.2 = (f32[80,128]{1,0:T(8,128)}, f32[80,128]{1,0:T(8,128)}, u32[]{:S(2)}, u32[]{:S(2)}) collective-permute-start(f32[80,128]{1,0:T(8,128)} %get-tuple-element.16), channel_id=1, source_target_pairs={{0,8},{8,16},{16,24},{24,32},{32,40},{40,48},{48,56},{56,64},{64,7... | collective-permute-start | bytes 122888 | tf_op jit(solution)/shard_map/ppermute | solution.py:250
  43.9 1.3 collective-permute-start.3
  45.2 8.1 %collective-permute-start = (f32[152,128]{1,0:T(8,128)}, f32[152,128]{1,0:T(8,128)}, u32[]{:S(2)}, u32[]{:S(2)}) collective-permute-start(f32[152,128]{1,0:T(8,128)} %get-tuple-element.14), channel_id=1, source_target_pairs={{0,1},{1,2},{2,3},{3,4},{4,5},{5,6},{6,7},{8,9},{9,10},{10,11},{11... | collective-permute-start | bytes 233480 | tf_op jit(solution)/shard_map/ppermute | solution.py:250
  53.4 1.9 %collective-permute-start.1 = (f32[152,128]{1,0:T(8,128)}, f32[152,128]{1,0:T(8,128)}, u32[]{:S(2)}, u32[]{:S(2)}) collective-permute-start(f32[152,128]{1,0:T(8,128)} %get-tuple-element.15), channel_id=1, source_target_pairs={{1,0},{2,1},{3,2},{4,3},{5,4},{6,5},{7,6},{9,8},{10,9},{11,10},{12... | collective-permute-start | bytes 233480 | tf_op jit(solution)/shard_map/ppermute | solution.py:250
  55.3 0.8 fusion
  56.1 0.1 reshape.37.wet_ref
  56.1 0.0 copy-done.7
  56.1 0.9 reshape.32
  57.0 1.8 copy.16
  58.8 1.2 reshape.33.index_ref
  60.1 1.8 copy.19
  61.8 0.0 collective-permute-done.2.west_ref
  61.8 0.0 collective-permute-done.3.east_ref
  61.8 0.0 collective-permute-done.south_ref
  61.8 4.5 %collective-permute-done.1.north_ref = f32[152,128]{1,0:T(8,128)} collective-permute-done((f32[152,128]{1,0:T(8,128)}, f32[152,128]{1,0:T(8,128)}, u32[]{:S(2)}, u32[]{:S(2)}) %collective-permute-start.1) | collective-permute-done | bytes 77856 | tf_op jit(solution)/shard_map/ppermute | solution.py:250
  66.3 0.0 copy-done.1
  66.3 0.0 copy-start.2
  66.3 1.1 copy-done.2
  67.4 0.0 copy-start.6
  67.4 0.9 copy-done.6
  68.3 0.0 copy-start.3
  68.3 23.4 %step.1 = (f32[1152,128]{1,0:T(8,128)S(1)}, f32[32,128]{1,0:T(8,128)S(1)}, f32[152,128]{1,0:T(8,128)S(1)}, f32[152,128]{1,0:T(8,128)S(1)}, f32[80,128]{1,0:T(8,128)S(1)}, /*index=5*/f32[80,128]{1,0:T(8,128)S(1)}) custom-call(s32[4608]{0:T(1024)S(1)} %reshape.33.index_ref, f32[1152,128]{1,0:T(8,128)S(1)} %bitcast.19, f32[32,128]{1,0:T(8,128)S(1)} %reshape.36.f_ref.f_in_ref, ...), custom_call_target="tpu_custom_call" | custom-call | tf_op jit(solution)/shard_map/step/pallas_call | solution.py:291
  91.7 5.5 %collective-permute-start.4 = (f32[152,128]{1,0:T(8,128)S(1)}, f32[152,128]{1,0:T(8,128)S(1)}, u32[]{:S(2)}, u32[]{:S(2)}) collective-permute-start(f32[152,128]{1,0:T(8,128)S(1)} %get-tuple-element.20), channel_id=1, source_target_pairs={{0,1},{1,2},{2,3},{3,4},{4,5},{5,6},{6,7},{8,9},{9,10},{10,11},{11... | collective-permute-start | bytes 233480 | tf_op jit(solution)/shard_map/ppermute | solution.py:250
  97.2 1.9 %collective-permute-start.5 = (f32[152,128]{1,0:T(8,128)S(1)}, f32[152,128]{1,0:T(8,128)S(1)}, u32[]{:S(2)}, u32[]{:S(2)}) collective-permute-start(f32[152,128]{1,0:T(8,128)S(1)} %get-tuple-element.21), channel_id=1, source_target_pairs={{1,0},{2,1},{3,2},{4,3},{5,4},{6,5},{7,6},{9,8},{10,9},{11,10},{12... | collective-permute-start | bytes 233480 | tf_op jit(solution)/shard_map/ppermute | solution.py:250
  99.1 2.8 %collective-permute-start.6 = (f32[80,128]{1,0:T(8,128)S(1)}, f32[80,128]{1,0:T(8,128)S(1)}, u32[]{:S(2)}, u32[]{:S(2)}) collective-permute-start(f32[80,128]{1,0:T(8,128)S(1)} %get-tuple-element.22), channel_id=1, source_target_pairs={{0,8},{8,16},{16,24},{24,32},{32,40},{40,48},{48,56},{56,64},{64,7... | collective-permute-start | bytes 122888 | tf_op jit(solution)/shard_map/ppermute | solution.py:250
  101.9 1.3 collective-permute-start.7
  103.2 0.0 collective-permute-done.6.west_ref
  103.2 3.9 %collective-permute-done.7.east_ref = f32[80,128]{1,0:T(8,128)S(1)} collective-permute-done((f32[80,128]{1,0:T(8,128)S(1)}, f32[80,128]{1,0:T(8,128)S(1)}, u32[]{:S(2)}, u32[]{:S(2)}) %collective-permute-start.7) | collective-permute-done | bytes 40992 | tf_op jit(solution)/shard_map/ppermute | solution.py:250
  107.1 0.0 collective-permute-done.4.south_ref
  107.1 3.1 %collective-permute-done.5.north_ref = f32[152,128]{1,0:T(8,128)S(1)} collective-permute-done((f32[152,128]{1,0:T(8,128)S(1)}, f32[152,128]{1,0:T(8,128)S(1)}, u32[]{:S(2)}, u32[]{:S(2)}) %collective-permute-start.5) | collective-permute-done | bytes 77856 | tf_op jit(solution)/shard_map/ppermute | solution.py:250
  110.2 0.0 copy-done.3
  110.3 22.6 %last_step.1 = (f32[1152,128]{1,0:T(8,128)}, f32[32,128]{1,0:T(8,128)S(1)}) custom-call(s32[4608]{0:T(1024)S(1)} %reshape.33.index_ref, f32[1152,128]{1,0:T(8,128)S(1)} %get-tuple-element.18.e_in_ref, f32[32,128]{1,0:T(8,128)S(1)} %get-tuple-element.19.f_in_ref, f32[1,128]{1,0:T(1,128)S(1)} %reshape.37.wet_ref, f32[1152,2]{1,0:T(8,128)S(1)} %bitcast.21, ...), custom_call_target="tpu_custom_call" | custom-call | tf_op jit(solution)/shard_map/last_step/pallas_call | solution.py:291
  132.9 14.9 %all_to_all.15 = f32[256,1,128]{2,1,0:T(1,128)S(1)} all-to-all(f32[256,1,128]{2,1,0:T(1,128)S(1)} %bitcast.25), channel_id=1, replica_groups=mesh['comp'=64,'grp'=8] {'grp'}, dimensions={0} | all-to-all | bytes 262144 | tf_op jit(solution)/shard_map/all_to_all | solution.py:240
  147.8 11.5 %all-to-all-start.1 = ((f32[1152,1,128]{2,1,0:T(1,128)}), f32[1152,1,128]{2,1,0:T(1,128)S(1)}, u32[]{:S(2)}, u32[]{:S(2)}) async-start(f32[1152,1,128]{2,1,0:T(1,128)} %bitcast.6), calls=%async_computation.1 | async-start | bytes 1179648 | tf_op jit(solution)/shard_map/all_to_all | solution.py:240
  159.3 0.5 broadcast.4
  159.8 0.9 reduce.3
  160.8 0.3 reshape_reshape.7
  161.1 0.1 copy_bitcast_fusion
  161.2 1.0 copy.22
  162.2 16.2 %all-to-all-done.1 = f32[1152,1,128]{2,1,0:T(1,128)S(1)} async-done(((f32[1152,1,128]{2,1,0:T(1,128)}), f32[1152,1,128]{2,1,0:T(1,128)S(1)}, u32[]{:S(2)}, u32[]{:S(2)}) %all-to-all-start.1) | async-done | bytes 589856 | tf_op jit(solution)/shard_map/all_to_all | solution.py:240
  178.5 4.9 %from_points.1 = f32[18,8,1024]{2,1,0:T(8,128)} custom-call(f32[1152,128]{1,0:T(8,128)S(1)} %bitcast.23), custom_call_target="tpu_custom_call" | custom-call | tf_op jit(solution)/shard_map/from_points/pallas_call | solution.py:301
  (1 shorter events, 0.0 us)
Async XLA Ops:
  0.6 19.8 %copy-start = (f32[2,16,64,16]{2,3,1,0:T(8,128)S(1)}, f32[2,16,64,16]{2,3,1,0:T(8,128)}, u32[]{:S(2)}) copy-start(f32[2,16,64,16]{2,3,1,0:T(8,128)} %param.13) | copy-start | bytes 393220
  0.6 1.1 copy-start.5
  1.8 54.4 %copy-start.7 = (s32[4,1152]{1,0:T(4,128)S(1)}, s32[4,1152]{1,0:T(4,128)}, u32[]{:S(2)}) copy-start(s32[4,1152]{1,0:T(4,128)} %param.10) | copy-start | bytes 55300
  5.8 0.8 copy-start.4
  6.7 59.7 %copy-start.1 = (bf16[1152,1152]{1,0:T(8,128)(2,1)S(1)}, bf16[1152,1152]{1,0:T(8,128)(2,1)}, u32[]{:S(2)}) copy-start(bf16[1152,1152]{1,0:T(8,128)(2,1)} %coupling_ref.3) | copy-start | bytes 7962628
  6.7 33.0 %all-to-all-start = ((f32[1152,1,128]{2,1,0:T(1,128)}), f32[1152,1,128]{2,1,0:T(1,128)S(1)}, u32[]{:S(2)}, u32[]{:S(2)}) async-start(f32[1152,1,128]{2,1,0:T(1,128)} %bitcast.22), calls=%async_computation | async-start | bytes 1179648 | tf_op jit(solution)/shard_map/all_to_all | solution.py:240
  41.5 20.3 %collective-permute-start.2 = (f32[80,128]{1,0:T(8,128)}, f32[80,128]{1,0:T(8,128)}, u32[]{:S(2)}, u32[]{:S(2)}) collective-permute-start(f32[80,128]{1,0:T(8,128)} %get-tuple-element.16), channel_id=1, source_target_pairs={{0,8},{8,16},{16,24},{24,32},{32,40},{40,48},{48,56},{56,64},{64,7... | collective-permute-start | bytes 122888 | tf_op jit(solution)/shard_map/ppermute | solution.py:250
  43.9 17.9 %collective-permute-start.3 = (f32[80,128]{1,0:T(8,128)}, f32[80,128]{1,0:T(8,128)}, u32[]{:S(2)}, u32[]{:S(2)}) collective-permute-start(f32[80,128]{1,0:T(8,128)} %get-tuple-element.17), channel_id=1, source_target_pairs={{8,0},{16,8},{24,16},{32,24},{40,32},{48,40},{56,48},{64,56},{72,6... | collective-permute-start | bytes 122888 | tf_op jit(solution)/shard_map/ppermute | solution.py:250
  45.2 16.6 %collective-permute-start = (f32[152,128]{1,0:T(8,128)}, f32[152,128]{1,0:T(8,128)}, u32[]{:S(2)}, u32[]{:S(2)}) collective-permute-start(f32[152,128]{1,0:T(8,128)} %get-tuple-element.14), channel_id=1, source_target_pairs={{0,1},{1,2},{2,3},{3,4},{4,5},{5,6},{6,7},{8,9},{9,10},{10,11},{11... | collective-permute-start | bytes 233480 | tf_op jit(solution)/shard_map/ppermute | solution.py:250
  53.4 12.9 %collective-permute-start.1 = (f32[152,128]{1,0:T(8,128)}, f32[152,128]{1,0:T(8,128)}, u32[]{:S(2)}, u32[]{:S(2)}) collective-permute-start(f32[152,128]{1,0:T(8,128)} %get-tuple-element.15), channel_id=1, source_target_pairs={{1,0},{2,1},{3,2},{4,3},{5,4},{6,5},{7,6},{9,8},{10,9},{11,10},{12... | collective-permute-start | bytes 233480 | tf_op jit(solution)/shard_map/ppermute | solution.py:250
  66.3 1.1 copy-start.2
  67.4 0.9 copy-start.6
  68.3 42.0 %copy-start.3 = (f32[2,1152]{0,1:T(8,128)S(1)}, f32[2,1152]{0,1:T(8,128)}, u32[]{:S(2)}) copy-start(f32[2,1152]{0,1:T(8,128)} %copy.19) | copy-start | bytes 27652
  91.7 15.5 %collective-permute-start.4 = (f32[152,128]{1,0:T(8,128)S(1)}, f32[152,128]{1,0:T(8,128)S(1)}, u32[]{:S(2)}, u32[]{:S(2)}) collective-permute-start(f32[152,128]{1,0:T(8,128)S(1)} %get-tuple-element.20), channel_id=1, source_target_pairs={{0,1},{1,2},{2,3},{3,4},{4,5},{5,6},{6,7},{8,9},{9,10},{10,11},{11... | collective-permute-start | bytes 233480 | tf_op jit(solution)/shard_map/ppermute | solution.py:250
  97.2 13.1 %collective-permute-start.5 = (f32[152,128]{1,0:T(8,128)S(1)}, f32[152,128]{1,0:T(8,128)S(1)}, u32[]{:S(2)}, u32[]{:S(2)}) collective-permute-start(f32[152,128]{1,0:T(8,128)S(1)} %get-tuple-element.21), channel_id=1, source_target_pairs={{1,0},{2,1},{3,2},{4,3},{5,4},{6,5},{7,6},{9,8},{10,9},{11,10},{12... | collective-permute-start | bytes 233480 | tf_op jit(solution)/shard_map/ppermute | solution.py:250
  99.1 4.1 %collective-permute-start.6 = (f32[80,128]{1,0:T(8,128)S(1)}, f32[80,128]{1,0:T(8,128)S(1)}, u32[]{:S(2)}, u32[]{:S(2)}) collective-permute-start(f32[80,128]{1,0:T(8,128)S(1)} %get-tuple-element.22), channel_id=1, source_target_pairs={{0,8},{8,16},{16,24},{24,32},{32,40},{40,48},{48,56},{56,64},{64,7... | collective-permute-start | bytes 122888 | tf_op jit(solution)/shard_map/ppermute | solution.py:250
  101.9 5.2 %collective-permute-start.7 = (f32[80,128]{1,0:T(8,128)S(1)}, f32[80,128]{1,0:T(8,128)S(1)}, u32[]{:S(2)}, u32[]{:S(2)}) collective-permute-start(f32[80,128]{1,0:T(8,128)S(1)} %get-tuple-element.23), channel_id=1, source_target_pairs={{8,0},{16,8},{24,16},{32,24},{40,32},{48,40},{56,48},{64,56},{72,6... | collective-permute-start | bytes 122888 | tf_op jit(solution)/shard_map/ppermute | solution.py:250
  147.8 30.7 %all-to-all-start.1 = ((f32[1152,1,128]{2,1,0:T(1,128)}), f32[1152,1,128]{2,1,0:T(1,128)S(1)}, u32[]{:S(2)}, u32[]{:S(2)}) async-start(f32[1152,1,128]{2,1,0:T(1,128)} %bitcast.6), calls=%async_computation.1 | async-start | bytes 1179648 | tf_op jit(solution)/shard_map/all_to_all | solution.py:240

commit v2 on v1

--- a/solution.py
+++ b/solution.py
@@ -58,7 +58,7 @@
             o_ref[pl.ds(j * 8 * parts + k, 8, stride=parts), :] = tile
         return carry
 
-    lax.fori_loop(0, parts, one, 0)
+    lax.fori_loop(0, parts, one, 0, unroll=3)
 
 
 def from_points_kernel(x_ref, o_ref):
@@ -70,7 +70,7 @@
             o_ref[k, :, j * LANES : (j + 1) * LANES] = exchange_blocks(tile)
         return carry
 
-    lax.fori_loop(0, parts, one, 0)
+    lax.fori_loop(0, parts, one, 0, unroll=3)
 
 
 def tile_rows(start, count=8):
@@ -153,12 +153,14 @@
     drift_y = jnp.broadcast_to(CURRENT_GAIN * jnp.tanh(f_in_ref[L : L + 1, :]), (8, LANES))
 
     def advect(m, carry):
+        group = pl.ds(pl.multiple_of(m * 128, 128), 128)
+        speed_x = jnp.broadcast_to(speed_ref[0:1, group], (128, LANES)).T
+        speed_y = jnp.broadcast_to(speed_ref[1:2, group], (128, LANES)).T
         for n in range(16):
             rows = tile_rows(m * 128 + n * 8)
             tile = e_in_ref[rows, :]
-            speed = speed_ref[rows, :]
-            a_x = speed[:, 0:1] + drift_x
-            a_y = speed[:, 1:2] + drift_y
+            a_x = speed_x[n * 8 : n * 8 + 8] + drift_x
+            a_y = speed_y[n * 8 : n * 8 + 8] + drift_y
             west, east, south, north = neighbours(tile, n, m, *halos)
             moved = (
                 tile
@@ -175,26 +177,21 @@
     sub = lax.broadcasted_iota(jnp.int32, (8, LANES), 0)
     here = [sub == s for s in range(8)]
 
-    def gathered(base):
+    def gathered(quad):
         picked = []
         for j in range(4):
             rows = None
             for s in range(8):
-                row = e_ref[pl.ds(index_ref[base + j * 8 + s], 8, stride=0), :]
+                row = e_ref[pl.ds(index_ref[j, quad + s], 8, stride=0), :]
                 rows = row if rows is None else jnp.where(here[s], row, rows)
             picked.append(rows)
         first, second, third, fourth = picked
         return first * second * (third + fourth) - third * fourth * (first + second)
 
-    def interactions(i, carry):
-        for t in range(2):
-            base = i * 128 + t * 64
-            both = jnp.concatenate([gathered(base), gathered(base + 32)], axis=0)
-            inter_ref[pl.ds(pl.multiple_of(i * 32 + t * 16, 16), 16), :] = both.astype(jnp.bfloat16)
-        return carry
-
     def substep(_, carry):
-        lax.fori_loop(0, quads // 32, interactions, 0)
+        for quad in range(0, quads, 16):
+            both = jnp.concatenate([gathered(quad), gathered(quad + 8)], axis=0)
+            inter_ref[quad : quad + 16, :] = both.astype(jnp.bfloat16)
         growth = jnp.dot(coupling_ref[...], inter_ref[...], preferred_element_type=jnp.float32)
         gained = SOURCE_GAIN * growth / (1.0 + SOURCE_GAIN * jnp.abs(growth))
         e_ref[0:channels, :] = e_ref[0:channels, :] + wet_ref[...] * gained
@@ -236,9 +233,21 @@
 
 
 def exchange(values, axis):
-    rows, lanes = values.shape
-    moved = lax.all_to_all(values.reshape(rows, 1, lanes), axis, split_axis=0, concat_axis=0, tiled=True)
-    return moved.reshape(rows, lanes)
+    peers = lax.axis_size(axis)
+    lines = values.reshape(peers, 1, values.size // peers)
+    moved = lax.all_to_all(lines, axis, split_axis=0, concat_axis=0, tiled=True)
+    return moved.reshape(values.shape)
+
+
+def gather_tiles(flow, groups, group_place):
+    held = flow[None]
+    bit = groups // 2
+    while bit:
+        other = lax.ppermute(held, "grp", [(i, i ^ bit) for i in range(groups)])
+        upper = (group_place & bit) != 0
+        held = jnp.concatenate([jnp.where(upper, other, held), jnp.where(upper, held, other)], axis=0)
+        bit //= 2
+    return held
 
 
 def send_edges(edges):
@@ -274,13 +283,11 @@
     wet_rows = (sea_mask == 1).astype(jnp.float32)
     wet = lax.dynamic_slice_in_dim(wet_rows, comp_place * cols_local, cols_local, 1).reshape(1, LANES)
     flow = lax.dynamic_slice_in_dim(ocean_flow, group_place * rows_local, rows_local, 2).reshape(FIELDS, LANES)
-    index = quad_index.reshape(4, quads // 8, 8).transpose(1, 0, 2).reshape(4 * quads)
-    speed = group_speed.T
 
     sent = pl.pallas_call(
         to_points_kernel, out_shape=float_of(channels, LANES), in_specs=[VMEM], out_specs=VMEM, compiler_params=SMALL, name="to_points"
     )(spectrum)
-    energy = exchange(sent, "comp")
+    energy, wet, flow = lax.optimization_barrier((exchange(sent, "comp"), wet, flow))
     edges = pl.pallas_call(
         edges_kernel, out_shape=edge_shapes, in_specs=[VMEM] * 2, out_specs=[VMEM] * 4, compiler_params=SMALL, name="edges"
     )(energy, flow)
@@ -296,7 +303,7 @@
             scratch_shapes=[pltpu.VMEM((channels + 8, LANES), jnp.float32), pltpu.VMEM((quads, LANES), jnp.bfloat16)],
             compiler_params=SMALL,
             name="last_step" if last else "step",
-        )(index, energy, flow, wet, speed, coupling, stokes_kernel, *halos)
+        )(quad_index, energy, flow, wet, group_speed, coupling, stokes_kernel, *halos)
     returned = exchange(energy, "comp")
     forecast = pl.pallas_call(
         from_points_kernel,
@@ -306,9 +313,10 @@
         compiler_params=SMALL,
         name="from_points",
     )(returned)
-    copies = jnp.broadcast_to(flow[None], (groups, FIELDS, LANES)).reshape(groups * FIELDS, LANES)
-    rows = exchange(copies, "grp").reshape(groups, 2, L, rows_local, cols_local)
-    ocean = rows.transpose(1, 2, 0, 3, 4).reshape(2, L, groups * rows_local, cols_local)
+    bits = groups.bit_length() - 1
+    tiles = gather_tiles(flow, groups, group_place).reshape((2,) * bits + (2, L, rows_local, cols_local))
+    order = (bits, bits + 1) + tuple(range(bits - 1, -1, -1)) + (bits + 2, bits + 3)
+    ocean = tiles.transpose(order).reshape(2, L, groups * rows_local, cols_local)
     return forecast, ocean
 
 

time: 187 us -> 152 us (0.81); the launches traced: 183 us -> 150 us
  Pallas kernels: 56.8 us -> 36.3 us
  blocking collectives: 14.9 us -> 0 us
  starting transfers between devices: 50.6 us -> 54.8 us
  local copies, waits for them, and re-layouts: 15.2 us -> 12 us
  waiting for transfers between devices: 43.3 us -> 45.6 us
    ppermute x0 -> x3, waiting for transfers between devices: none -> 19 us  [gather_tiles(): other = lax.ppermute(held, 'grp', [(i, i ^ bit) for i in range(groups)])]
    all_to_all x2, waiting for transfers between devices: 31.8 us -> 14.2 us  [exchange(): moved = lax.all_to_all(lines, axis, split_axis=0, concat_axis=0, tiled=True)]
    all_to_all x1 -> x0, blocking collectives: 14.9 us -> none  [exchange(): lax.all_to_all(values.reshape(rows, 1, lanes), axis, split_axis=0, concat...]
    pallas_call x2, Pallas kernels: 46 us -> 31.2 us  [local(): pl.pallas_call(functools.partial(step_kernel, last), out_shape=outs, in_s...]
    ppermute x0 -> x3, starting transfers between devices: none -> 5.76 us  [gather_tiles(): other = lax.ppermute(held, 'grp', [(i, i ^ bit) for i in range(groups)])]
    pallas_call x1, Pallas kernels: 4.08 us -> 1.57 us  [local(): pl.pallas_call(to_points_kernel, out_shape=float_of(channels, LANES), in_...]
    pallas_call x1, Pallas kernels: 4.89 us -> 2.39 us  [local(): pl.pallas_call(from_points_kernel, out_shape=float_of(parts, rows_local,...]
    all_to_all x2, starting transfers between devices: 25.3 us -> 23 us  [exchange(): moved = lax.all_to_all(lines, axis, split_axis=0, concat_axis=0, tiled=True)]
  transfers between devices with their start and end apart: 10 -> 13, of which waited for: 5 -> 8; matrix products, arithmetic and copies ran while one was open for 7% -> 6% of each run, Pallas kernels for 0% -> 0%
where the time goes in v2:
time: 152 us; the launch traced here: 150 us
  starting transfers between devices  54.8 us (36%)
  waiting for transfers between devices  45.6 us (30%)
  Pallas kernels  36.3 us (24%)
  local copies, waits for them, and re-layouts  12 us (8%)
    pallas_call x2, Pallas kernels, local(): pl.pallas_call(functools.partial(step_kernel, last), out_shape=outs, in_s...  31.2 us
    ppermute x8, starting transfers between devices, shift(): return lax.ppermute(value, axis, pairs)  26.1 us
    all_to_all x2, starting transfers between devices, exchange(): moved = lax.all_to_all(lines, axis, split_axis=0, concat_axis=0, tiled=True)  23 us
    ppermute x3, waiting for transfers between devices, gather_tiles(): other = lax.ppermute(held, 'grp', [(i, i ^ bit) for i in range(groups)])  19 us
    all_to_all x2, waiting for transfers between devices, exchange(): moved = lax.all_to_all(lines, axis, split_axis=0, concat_axis=0, tiled=True)  14.2 us
    ppermute x8, waiting for transfers between devices, shift(): return lax.ppermute(value, axis, pairs)  12.4 us
    ppermute x3, starting transfers between devices, gather_tiles(): other = lax.ppermute(held, 'grp', [(i, i ^ bit) for i in range(groups)])  5.76 us
    unnamed x21, local copies, waits for them, and re-layouts  5.17 us
  transfers between devices with their start and end apart: 13, of which 8 were waited for; matrix products, arithmetic and copies ran while one was open for 6% of the time, Pallas kernels for 0%

profile of v2, /device:TPU:6, one launch (start us, length us, event | category | flops | bytes accessed | tf_op | source)
XLA Modules:
  0.0 150.4 jit_solution(5136526998637007144)
XLA Ops:
  0.6 0.0 copy-start
  0.6 0.0 copy-start.1
  0.7 0.0 copy-start.5
  0.7 1.2 copy-done.5
  1.9 0.0 copy-start.6
  1.9 0.0 copy-start.7
  1.9 1.6 %to_points.1 = f32[1152,128]{1,0:T(8,128)S(1)} custom-call(f32[18,8,1024]{2,1,0:T(8,128)S(1)} %copy-done.5), custom_call_target="tpu_custom_call" | custom-call | tf_op jit(solution)/shard_map/to_points/pallas_call | solution.py:287
  3.5 0.0 copy-start.2
  3.5 0.8 copy-done.2
  4.3 13.5 %all-to-all-start = ((f32[64,1,2304]{2,1,0:T(1,128)}), f32[64,1,2304]{2,1,0:T(1,128)S(1)}, u32[]{:S(2)}, u32[]{:S(2)}) async-start(f32[64,1,2304]{2,1,0:T(1,128)} %bitcast.15), calls=%async_computation | async-start | bytes 1179648 | tf_op jit(solution)/shard_map/all_to_all | solution.py:238
  17.8 0.8 fusion
  18.6 0.6 reshape.30.wet_ref
  19.2 0.0 copy-done
  19.2 0.8 constant_dynamic-slice_fusion
  20.0 1.7 %copy.15 = f32[2,16,8,16]{3,2,1,0:T(8,128)} copy(f32[2,16,8,16]{2,3,1,0:T(8,128)} %constant_dynamic-slice_fusion) | data formatting | bytes 32768 | tf_op jit(solution)/shard_map/dynamic_slice | solution.py:285
  21.7 1.0 reshape.31.f_ref.f_in_ref
  22.7 14.2 %all-to-all-done = f32[64,1,2304]{2,1,0:T(1,128)S(1)} async-done(((f32[64,1,2304]{2,1,0:T(1,128)}), f32[64,1,2304]{2,1,0:T(1,128)S(1)}, u32[]{:S(2)}, u32[]{:S(2)}) %all-to-all-start) | async-done | bytes 589856 | tf_op jit(solution)/shard_map/all_to_all | solution.py:238
  37.0 0.0 copy-start.4
  37.0 1.2 edges.1
  38.2 8.1 %collective-permute-start = (f32[152,128]{1,0:T(8,128)S(1)}, f32[152,128]{1,0:T(8,128)S(1)}, u32[]{:S(2)}, u32[]{:S(2)}) collective-permute-start(f32[152,128]{1,0:T(8,128)S(1)} %get-tuple-element.20), channel_id=1, source_target_pairs={{0,1},{1,2},{2,3},{3,4},{4,5},{5,6},{6,7},{8,9},{9,10},{10,11},{11... | collective-permute-start | bytes 233480 | tf_op jit(solution)/shard_map/ppermute | solution.py:259
  46.4 1.9 %collective-permute-start.1 = (f32[152,128]{1,0:T(8,128)S(1)}, f32[152,128]{1,0:T(8,128)S(1)}, u32[]{:S(2)}, u32[]{:S(2)}) collective-permute-start(f32[152,128]{1,0:T(8,128)S(1)} %get-tuple-element.21), channel_id=1, source_target_pairs={{1,0},{2,1},{3,2},{4,3},{5,4},{6,5},{7,6},{9,8},{10,9},{11,10},{12... | collective-permute-start | bytes 233480 | tf_op jit(solution)/shard_map/ppermute | solution.py:259
  48.3 1.5 collective-permute-start.2
  49.8 1.3 collective-permute-start.3
  51.1 0.0 collective-permute-done.2.west_ref
  51.1 3.3 %collective-permute-done.3.east_ref = f32[80,128]{1,0:T(8,128)S(1)} collective-permute-done((f32[80,128]{1,0:T(8,128)S(1)}, f32[80,128]{1,0:T(8,128)S(1)}, u32[]{:S(2)}, u32[]{:S(2)}) %collective-permute-start.3) | collective-permute-done | bytes 40992 | tf_op jit(solution)/shard_map/ppermute | solution.py:259
  54.4 0.0 collective-permute-done.south_ref
  54.4 4.3 %collective-permute-done.1.north_ref = f32[152,128]{1,0:T(8,128)S(1)} collective-permute-done((f32[152,128]{1,0:T(8,128)S(1)}, f32[152,128]{1,0:T(8,128)S(1)}, u32[]{:S(2)}, u32[]{:S(2)}) %collective-permute-start.1) | collective-permute-done | bytes 77856 | tf_op jit(solution)/shard_map/ppermute | solution.py:259
  58.7 0.0 copy-done.1
  58.7 0.0 copy-done.6
  58.7 0.0 copy-done.7
  58.7 0.0 copy-start.3
  58.7 0.9 copy-done.3
  59.6 0.0 copy-start.8
  59.6 0.6 copy-done.8
  60.2 15.9 %step.1 = (f32[1152,128]{1,0:T(8,128)S(1)}, f32[32,128]{1,0:T(8,128)S(1)}, f32[152,128]{1,0:T(8,128)S(1)}, f32[152,128]{1,0:T(8,128)S(1)}, f32[80,128]{1,0:T(8,128)S(1)}, /*index=5*/f32[80,128]{1,0:T(8,128)S(1)}) custom-call(s32[4,1152]{1,0:T(4,128)S(1)} %copy-done.6, f32[1152,128]{1,0:T(8,128)S(1)} %bitcast.13, f32[32,128]{1,0:T(8,128)S(1)} %reshape.31.f_ref.f_in_ref, ...), custom_call_target="tpu_custom_call" | custom-call | tf_op jit(solution)/shard_map/step/pallas_call | solution.py:298
  76.1 5.7 %collective-permute-start.4 = (f32[152,128]{1,0:T(8,128)S(1)}, f32[152,128]{1,0:T(8,128)S(1)}, u32[]{:S(2)}, u32[]{:S(2)}) collective-permute-start(f32[152,128]{1,0:T(8,128)S(1)} %get-tuple-element.26), channel_id=1, source_target_pairs={{0,1},{1,2},{2,3},{3,4},{4,5},{5,6},{6,7},{8,9},{9,10},{10,11},{11... | collective-permute-start | bytes 233480 | tf_op jit(solution)/shard_map/ppermute | solution.py:259
  81.8 1.9 %collective-permute-start.5 = (f32[152,128]{1,0:T(8,128)S(1)}, f32[152,128]{1,0:T(8,128)S(1)}, u32[]{:S(2)}, u32[]{:S(2)}) collective-permute-start(f32[152,128]{1,0:T(8,128)S(1)} %get-tuple-element.27), channel_id=1, source_target_pairs={{1,0},{2,1},{3,2},{4,3},{5,4},{6,5},{7,6},{9,8},{10,9},{11,10},{12... | collective-permute-start | bytes 233480 | tf_op jit(solution)/shard_map/ppermute | solution.py:259
  83.7 4.3 %collective-permute-start.6 = (f32[80,128]{1,0:T(8,128)S(1)}, f32[80,128]{1,0:T(8,128)S(1)}, u32[]{:S(2)}, u32[]{:S(2)}) collective-permute-start(f32[80,128]{1,0:T(8,128)S(1)} %get-tuple-element.28), channel_id=1, source_target_pairs={{0,8},{8,16},{16,24},{24,32},{32,40},{40,48},{48,56},{56,64},{64,7... | collective-permute-start | bytes 122888 | tf_op jit(solution)/shard_map/ppermute | solution.py:259
  88.1 1.3 collective-permute-start.7
  89.4 0.0 collective-permute-done.6.west_ref
  89.4 1.8 %collective-permute-done.7.east_ref = f32[80,128]{1,0:T(8,128)S(1)} collective-permute-done((f32[80,128]{1,0:T(8,128)S(1)}, f32[80,128]{1,0:T(8,128)S(1)}, u32[]{:S(2)}, u32[]{:S(2)}) %collective-permute-start.7) | collective-permute-done | bytes 40992 | tf_op jit(solution)/shard_map/ppermute | solution.py:259
  91.2 0.0 collective-permute-done.4.south_ref
  91.2 3.0 %collective-permute-done.5.north_ref = f32[152,128]{1,0:T(8,128)S(1)} collective-permute-done((f32[152,128]{1,0:T(8,128)S(1)}, f32[152,128]{1,0:T(8,128)S(1)}, u32[]{:S(2)}, u32[]{:S(2)}) %collective-permute-start.5) | collective-permute-done | bytes 77856 | tf_op jit(solution)/shard_map/ppermute | solution.py:259
  94.2 0.0 copy-done.4
  94.2 0.0 copy-start.9
  94.2 0.6 copy-done.9
  94.8 15.3 %last_step.1 = (f32[1152,128]{1,0:T(8,128)}, f32[32,128]{1,0:T(8,128)S(1)}) custom-call(s32[4,1152]{1,0:T(4,128)S(1)} %copy-done.6, f32[1152,128]{1,0:T(8,128)S(1)} %get-tuple-element.24.e_in_ref, f32[32,128]{1,0:T(8,128)S(1)} %get-tuple-element.25.f_in_ref, f32[1,128]{1,0:T(1,128)S(1)} %copy-done.9, f32[2,1152]{1,0:T(2,128)S(1)} %copy-done.7, ...), custom_call_target="tpu_custom_call" | custom-call | tf_op jit(solution)/shard_map/last_step/pallas_call | solution.py:298
  110.1 9.4 %all-to-all-start.1 = ((f32[64,1,2304]{2,1,0:T(1,128)}), f32[64,1,2304]{2,1,0:T(1,128)S(1)}, u32[]{:S(2)}, u32[]{:S(2)}) async-start(f32[64,1,2304]{2,1,0:T(1,128)} %bitcast.2), calls=%async_computation.1 | async-start | bytes 1179648 | tf_op jit(solution)/shard_map/all_to_all | solution.py:238
  119.5 1.9 %collective-permute-start.8 = (f32[1,32,128]{2,1,0:T(8,128)S(1)}, f32[1,32,128]{2,1,0:T(8,128)S(1)}, u32[]{:S(2)}, u32[]{:S(2)}) collective-permute-start(f32[1,32,128]{2,1,0:T(8,128)S(1)} %bitcast.16), channel_id=1, source_target_pairs={{0,4},{1,5},{2,6},{3,7},{4,0},{5,1},{6,2},{7,3},{8,12},{9,13},{10,... | collective-permute-start | bytes 49160 | tf_op jit(solution)/shard_map/ppermute | solution.py:246
  121.4 9.4 %collective-permute-done.8 = f32[1,32,128]{2,1,0:T(8,128)S(1)} collective-permute-done((f32[1,32,128]{2,1,0:T(8,128)S(1)}, f32[1,32,128]{2,1,0:T(8,128)S(1)}, u32[]{:S(2)}, u32[]{:S(2)}) %collective-permute-start.8) | collective-permute-done | bytes 16416 | tf_op jit(solution)/shard_map/ppermute | solution.py:246
  130.8 1.9 %collective-permute-start.9 = (f32[2,32,128]{2,1,0:T(8,128)S(1)}, f32[2,32,128]{2,1,0:T(8,128)S(1)}, u32[]{:S(2)}, u32[]{:S(2)}) collective-permute-start(f32[2,32,128]{2,1,0:T(8,128)S(1)} %pad_maximum_fusion.2), channel_id=1, source_target_pairs={{0,2},{1,3},{2,0},{3,1},{4,6},{5,7},{6,4},{7,5},{8,10},{9,11},{10,... | collective-permute-start | bytes 98312 | tf_op jit(solution)/shard_map/ppermute | solution.py:246
  132.7 5.4 %collective-permute-done.9 = f32[2,32,128]{2,1,0:T(8,128)S(1)} collective-permute-done((f32[2,32,128]{2,1,0:T(8,128)S(1)}, f32[2,32,128]{2,1,0:T(8,128)S(1)}, u32[]{:S(2)}, u32[]{:S(2)}) %collective-permute-start.9) | collective-permute-done | bytes 32800 | tf_op jit(solution)/shard_map/ppermute | solution.py:246
  138.2 1.9 %collective-permute-start.10 = (f32[4,32,128]{2,1,0:T(8,128)S(1)}, f32[4,32,128]{2,1,0:T(8,128)S(1)}, u32[]{:S(2)}, u32[]{:S(2)}) collective-permute-start(f32[4,32,128]{2,1,0:T(8,128)S(1)} %pad_maximum_fusion.1), channel_id=1, source_target_pairs={{0,1},{1,0},{2,3},{3,2},{4,5},{5,4},{6,7},{7,6},{8,9},{9,8},{10,11... | collective-permute-start | bytes 196616 | tf_op jit(solution)/shard_map/ppermute | solution.py:246
  140.1 4.2 %collective-permute-done.10 = f32[4,32,128]{2,1,0:T(8,128)S(1)} collective-permute-done((f32[4,32,128]{2,1,0:T(8,128)S(1)}, f32[4,32,128]{2,1,0:T(8,128)S(1)}, u32[]{:S(2)}, u32[]{:S(2)}) %collective-permute-start.10) | collective-permute-done | bytes 65568 | tf_op jit(solution)/shard_map/ppermute | solution.py:246
  144.3 1.3 reshape.34
  145.7 1.3 copy.17
  147.0 1.0 copy.18
  148.0 0.0 all-to-all-done.1
  148.0 2.4 %from_points.1 = f32[18,8,1024]{2,1,0:T(8,128)} custom-call(f32[1152,128]{1,0:T(8,128)S(1)} %bitcast.14), custom_call_target="tpu_custom_call" | custom-call | tf_op jit(solution)/shard_map/from_points/pallas_call | solution.py:308
  (6 shorter events, 0.0 us)
Async XLA Ops:
  0.6 18.5 %copy-start = (f32[2,16,64,16]{2,3,1,0:T(8,128)S(1)}, f32[2,16,64,16]{2,3,1,0:T(8,128)}, u32[]{:S(2)}) copy-start(f32[2,16,64,16]{2,3,1,0:T(8,128)} %param.13) | copy-start | bytes 393220
  0.6 58.0 %copy-start.1 = (bf16[1152,1152]{1,0:T(8,128)(2,1)S(1)}, bf16[1152,1152]{1,0:T(8,128)(2,1)}, u32[]{:S(2)}) copy-start(bf16[1152,1152]{1,0:T(8,128)(2,1)} %coupling_ref.3) | copy-start | bytes 7962628
  0.7 1.2 copy-start.5
  1.9 56.8 %copy-start.6 = (s32[4,1152]{1,0:T(4,128)S(1)}, s32[4,1152]{1,0:T(4,128)}, u32[]{:S(2)}) copy-start(s32[4,1152]{1,0:T(4,128)} %index_ref.3) | copy-start | bytes 55300
  1.9 56.8 %copy-start.7 = (f32[2,1152]{1,0:T(2,128)S(1)}, f32[2,1152]{1,0:T(2,128)}, u32[]{:S(2)}) copy-start(f32[2,1152]{1,0:T(2,128)} %speed_ref.3) | copy-start | bytes 27652
  3.5 0.8 copy-start.2
  4.3 32.7 %all-to-all-start = ((f32[64,1,2304]{2,1,0:T(1,128)}), f32[64,1,2304]{2,1,0:T(1,128)S(1)}, u32[]{:S(2)}, u32[]{:S(2)}) async-start(f32[64,1,2304]{2,1,0:T(1,128)} %bitcast.15), calls=%async_computation | async-start | bytes 1179648 | tf_op jit(solution)/shard_map/all_to_all | solution.py:238
  37.0 57.2 %copy-start.4 = (f32[32,1152]{1,0:T(8,128)S(1)}, f32[32,1152]{1,0:T(8,128)}, u32[]{:S(2)}) copy-start(f32[32,1152]{1,0:T(8,128)} %profile_ref.3) | copy-start | bytes 442372
  38.2 16.2 %collective-permute-start = (f32[152,128]{1,0:T(8,128)S(1)}, f32[152,128]{1,0:T(8,128)S(1)}, u32[]{:S(2)}, u32[]{:S(2)}) collective-permute-start(f32[152,128]{1,0:T(8,128)S(1)} %get-tuple-element.20), channel_id=1, source_target_pairs={{0,1},{1,2},{2,3},{3,4},{4,5},{5,6},{6,7},{8,9},{9,10},{10,11},{11... | collective-permute-start | bytes 233480 | tf_op jit(solution)/shard_map/ppermute | solution.py:259
  46.4 12.3 %collective-permute-start.1 = (f32[152,128]{1,0:T(8,128)S(1)}, f32[152,128]{1,0:T(8,128)S(1)}, u32[]{:S(2)}, u32[]{:S(2)}) collective-permute-start(f32[152,128]{1,0:T(8,128)S(1)} %get-tuple-element.21), channel_id=1, source_target_pairs={{1,0},{2,1},{3,2},{4,3},{5,4},{6,5},{7,6},{9,8},{10,9},{11,10},{12... | collective-permute-start | bytes 233480 | tf_op jit(solution)/shard_map/ppermute | solution.py:259
  48.3 2.8 %collective-permute-start.2 = (f32[80,128]{1,0:T(8,128)S(1)}, f32[80,128]{1,0:T(8,128)S(1)}, u32[]{:S(2)}, u32[]{:S(2)}) collective-permute-start(f32[80,128]{1,0:T(8,128)S(1)} %get-tuple-element.22), channel_id=1, source_target_pairs={{0,8},{8,16},{16,24},{24,32},{32,40},{40,48},{48,56},{56,64},{64,7... | collective-permute-start | bytes 122888 | tf_op jit(solution)/shard_map/ppermute | solution.py:259
  49.8 4.6 %collective-permute-start.3 = (f32[80,128]{1,0:T(8,128)S(1)}, f32[80,128]{1,0:T(8,128)S(1)}, u32[]{:S(2)}, u32[]{:S(2)}) collective-permute-start(f32[80,128]{1,0:T(8,128)S(1)} %get-tuple-element.23), channel_id=1, source_target_pairs={{8,0},{16,8},{24,16},{32,24},{40,32},{48,40},{56,48},{64,56},{72,6... | collective-permute-start | bytes 122888 | tf_op jit(solution)/shard_map/ppermute | solution.py:259
  58.7 0.9 copy-start.3
  59.6 0.6 copy-start.8
  76.1 15.1 %collective-permute-start.4 = (f32[152,128]{1,0:T(8,128)S(1)}, f32[152,128]{1,0:T(8,128)S(1)}, u32[]{:S(2)}, u32[]{:S(2)}) collective-permute-start(f32[152,128]{1,0:T(8,128)S(1)} %get-tuple-element.26), channel_id=1, source_target_pairs={{0,1},{1,2},{2,3},{3,4},{4,5},{5,6},{6,7},{8,9},{9,10},{10,11},{11... | collective-permute-start | bytes 233480 | tf_op jit(solution)/shard_map/ppermute | solution.py:259
  81.8 12.4 %collective-permute-start.5 = (f32[152,128]{1,0:T(8,128)S(1)}, f32[152,128]{1,0:T(8,128)S(1)}, u32[]{:S(2)}, u32[]{:S(2)}) collective-permute-start(f32[152,128]{1,0:T(8,128)S(1)} %get-tuple-element.27), channel_id=1, source_target_pairs={{1,0},{2,1},{3,2},{4,3},{5,4},{6,5},{7,6},{9,8},{10,9},{11,10},{12... | collective-permute-start | bytes 233480 | tf_op jit(solution)/shard_map/ppermute | solution.py:259
  83.7 5.6 %collective-permute-start.6 = (f32[80,128]{1,0:T(8,128)S(1)}, f32[80,128]{1,0:T(8,128)S(1)}, u32[]{:S(2)}, u32[]{:S(2)}) collective-permute-start(f32[80,128]{1,0:T(8,128)S(1)} %get-tuple-element.28), channel_id=1, source_target_pairs={{0,8},{8,16},{16,24},{24,32},{32,40},{40,48},{48,56},{56,64},{64,7... | collective-permute-start | bytes 122888 | tf_op jit(solution)/shard_map/ppermute | solution.py:259
  88.1 3.1 %collective-permute-start.7 = (f32[80,128]{1,0:T(8,128)S(1)}, f32[80,128]{1,0:T(8,128)S(1)}, u32[]{:S(2)}, u32[]{:S(2)}) collective-permute-start(f32[80,128]{1,0:T(8,128)S(1)} %get-tuple-element.29), channel_id=1, source_target_pairs={{8,0},{16,8},{24,16},{32,24},{40,32},{48,40},{56,48},{64,56},{72,6... | collective-permute-start | bytes 122888 | tf_op jit(solution)/shard_map/ppermute | solution.py:259
  94.2 0.6 copy-start.9
  110.1 38.0 %all-to-all-start.1 = ((f32[64,1,2304]{2,1,0:T(1,128)}), f32[64,1,2304]{2,1,0:T(1,128)S(1)}, u32[]{:S(2)}, u32[]{:S(2)}) async-start(f32[64,1,2304]{2,1,0:T(1,128)} %bitcast.2), calls=%async_computation.1 | async-start | bytes 1179648 | tf_op jit(solution)/shard_map/all_to_all | solution.py:238
  119.5 11.3 %collective-permute-start.8 = (f32[1,32,128]{2,1,0:T(8,128)S(1)}, f32[1,32,128]{2,1,0:T(8,128)S(1)}, u32[]{:S(2)}, u32[]{:S(2)}) collective-permute-start(f32[1,32,128]{2,1,0:T(8,128)S(1)} %bitcast.16), channel_id=1, source_target_pairs={{0,4},{1,5},{2,6},{3,7},{4,0},{5,1},{6,2},{7,3},{8,12},{9,13},{10,... | collective-permute-start | bytes 49160 | tf_op jit(solution)/shard_map/ppermute | solution.py:246
  130.8 7.3 %collective-permute-start.9 = (f32[2,32,128]{2,1,0:T(8,128)S(1)}, f32[2,32,128]{2,1,0:T(8,128)S(1)}, u32[]{:S(2)}, u32[]{:S(2)}) collective-permute-start(f32[2,32,128]{2,1,0:T(8,128)S(1)} %pad_maximum_fusion.2), channel_id=1, source_target_pairs={{0,2},{1,3},{2,0},{3,1},{4,6},{5,7},{6,4},{7,5},{8,10},{9,11},{10,... | collective-permute-start | bytes 98312 | tf_op jit(solution)/shard_map/ppermute | solution.py:246
  138.2 6.2 %collective-permute-start.10 = (f32[4,32,128]{2,1,0:T(8,128)S(1)}, f32[4,32,128]{2,1,0:T(8,128)S(1)}, u32[]{:S(2)}, u32[]{:S(2)}) collective-permute-start(f32[4,32,128]{2,1,0:T(8,128)S(1)} %pad_maximum_fusion.1), channel_id=1, source_target_pairs={{0,1},{1,0},{2,3},{3,2},{4,5},{5,4},{6,7},{7,6},{8,9},{9,8},{10,11... | collective-permute-start | bytes 196616 | tf_op jit(solution)/shard_map/ppermute | solution.py:246

commit v3 on v2

--- a/solution.py
+++ b/solution.py
@@ -77,7 +77,9 @@
     return pl.ds(start if isinstance(start, int) else pl.multiple_of(start, 8), count)
 
 
-def pack_group(load, count, m, up_ref, down_ref, east_ref, west_ref):
+def pack_group(load, count, m, odd_ref, rows_a_ref, rows_b_ref, cols_a_ref, cols_b_ref):
+    odd_row = odd_ref[0] == 1
+    odd_col = odd_ref[1] == 1
     block, col = lane_places()
     east = west = None
     for h in range((count + 7) // 8):
@@ -93,19 +95,19 @@
             down = d if down is None else jnp.where(block == i, d, down)
             east = e if east is None else jnp.where(col == n, e, east)
             west = w if west is None else jnp.where(col == n, w, west)
-        up_ref[tile_rows((2 * m + h) * 8), :] = up
-        down_ref[tile_rows((2 * m + h) * 8), :] = down
-    east_ref[tile_rows(m * 8), :] = east
-    west_ref[tile_rows(m * 8), :] = west
-
-
-def pack_all(e_ref, f_ref, channels, edges):
+        rows_a_ref[tile_rows((2 * m + h) * 8), :] = jnp.where(odd_row, down, up)
+        rows_b_ref[tile_rows((2 * m + h) * 8), :] = jnp.where(odd_row, up, down)
+    cols_a_ref[tile_rows(m * 8), :] = jnp.where(odd_col, west, east)
+    cols_b_ref[tile_rows(m * 8), :] = jnp.where(odd_col, east, west)
+
+
+def pack_all(e_ref, f_ref, channels, odd_ref, edges):
     def one(m, carry):
-        pack_group(lambda n: e_ref[tile_rows(m * 128 + n * 8), :], 16, m, *edges)
+        pack_group(lambda n: e_ref[tile_rows(m * 128 + n * 8), :], 16, m, odd_ref, *edges)
         return carry
 
     lax.fori_loop(0, channels // 128, one, 0)
-    pack_group(lambda n: f_ref[n * 8 : n * 8 + 8, :], FIELDS // 8, channels // 128, *edges)
+    pack_group(lambda n: f_ref[n * 8 : n * 8 + 8, :], FIELDS // 8, channels // 128, odd_ref, *edges)
 
 
 def neighbours(tile, n, m, south_ref, north_ref, west_ref, east_ref):
@@ -123,12 +125,13 @@
     )
 
 
-def edges_kernel(e_ref, f_ref, *edges):
-    pack_all(e_ref, f_ref, e_ref.shape[0], edges)
+def edges_kernel(odd_ref, e_ref, f_ref, *edges):
+    pack_all(e_ref, f_ref, e_ref.shape[0], odd_ref, edges)
 
 
 def step_kernel(
     last,
+    odd_ref,
     index_ref,
     e_in_ref,
     f_in_ref,
@@ -136,18 +139,24 @@
     speed_ref,
     coupling_ref,
     profile_ref,
-    south_ref,
-    north_ref,
-    west_ref,
-    east_ref,
+    rows_a_ref,
+    rows_b_ref,
+    cols_a_ref,
+    cols_b_ref,
     e_out_ref,
     f_out_ref,
     *rest,
 ):
-    edges, (e_ref, inter_ref) = rest[:-2], rest[-2:]
+    edges, (e_ref, inter_ref, *halos) = rest[:-6], rest[-6:]
     channels = e_in_ref.shape[0]
     quads = inter_ref.shape[0]
-    halos = (south_ref, north_ref, west_ref, east_ref)
+    odd_row = odd_ref[0] == 1
+    odd_col = odd_ref[1] == 1
+    south_ref, north_ref, west_ref, east_ref = halos
+    south_ref[...] = jnp.where(odd_row, rows_a_ref[...], rows_b_ref[...])
+    north_ref[...] = jnp.where(odd_row, rows_b_ref[...], rows_a_ref[...])
+    west_ref[...] = jnp.where(odd_col, cols_a_ref[...], cols_b_ref[...])
+    east_ref[...] = jnp.where(odd_col, cols_b_ref[...], cols_a_ref[...])
     wet = jnp.broadcast_to(wet_ref[...], (8, LANES))
     drift_x = jnp.broadcast_to(CURRENT_GAIN * jnp.tanh(f_in_ref[0:1, :]), (8, LANES))
     drift_y = jnp.broadcast_to(CURRENT_GAIN * jnp.tanh(f_in_ref[L : L + 1, :]), (8, LANES))
@@ -229,7 +238,7 @@
     f_out_ref[L : 2 * L, :] = flow_y - CORIOLIS * (flow_x + stokes_x) - vortex * stokes_x + mixed_y
 
     if not last:
-        pack_all(e_ref, f_out_ref, channels, edges)
+        pack_all(e_ref, f_out_ref, channels, odd_ref, edges)
 
 
 def exchange(values, axis):
@@ -239,30 +248,21 @@
     return moved.reshape(values.shape)
 
 
-def gather_tiles(flow, groups, group_place):
-    held = flow[None]
-    bit = groups // 2
-    while bit:
-        other = lax.ppermute(held, "grp", [(i, i ^ bit) for i in range(groups)])
-        upper = (group_place & bit) != 0
-        held = jnp.concatenate([jnp.where(upper, other, held), jnp.where(upper, held, other)], axis=0)
-        bit //= 2
-    return held
-
-
-def send_edges(edges):
-    up, down, east, west = edges
-
-    def shift(value, axis, by):
+def swap_edges(edges):
+    rows_a, rows_b, cols_a, cols_b = edges
+
+    def swap(value, axis, shift):
         count = lax.axis_size(axis)
-        pairs = [(i, i + by) for i in range(count) if 0 <= i + by < count]
-        return lax.ppermute(value, axis, pairs)
-
-    south = shift(up, "grp", 1)
-    north = shift(down, "grp", -1)
-    from_west = shift(east, "comp", 1)
-    from_east = shift(west, "comp", -1)
-    return south, north, from_west, from_east
+        partner = [((i + shift) ^ 1) - shift for i in range(count)]
+        return lax.ppermute(value, axis, [(i, j) for i, j in enumerate(partner) if 0 <= j < count])
+
+    from_b = swap(rows_b, "grp", 1)
+    from_a = swap(rows_a, "grp", 0)
+    return (from_a, from_b, swap(cols_b, "comp", 1), swap(cols_a, "comp", 0))
+
+
+def ordered(upper, mine, other):
+    return jnp.where(upper, other, mine), jnp.where(upper, mine, other)
 
 
 def local(spectrum, group_speed, sea_mask, quad_index, coupling, stokes_kernel, ocean_flow):
@@ -284,27 +284,35 @@
     wet = lax.dynamic_slice_in_dim(wet_rows, comp_place * cols_local, cols_local, 1).reshape(1, LANES)
     flow = lax.dynamic_slice_in_dim(ocean_flow, group_place * rows_local, rows_local, 2).reshape(FIELDS, LANES)
 
+    odd = jnp.stack([group_place & 1, comp_place & 1]).astype(jnp.int32)
+
     sent = pl.pallas_call(
         to_points_kernel, out_shape=float_of(channels, LANES), in_specs=[VMEM], out_specs=VMEM, compiler_params=SMALL, name="to_points"
     )(spectrum)
-    energy, wet, flow = lax.optimization_barrier((exchange(sent, "comp"), wet, flow))
+    energy, wet, flow, odd = lax.optimization_barrier((exchange(sent, "comp"), wet, flow, odd))
     edges = pl.pallas_call(
-        edges_kernel, out_shape=edge_shapes, in_specs=[VMEM] * 2, out_specs=[VMEM] * 4, compiler_params=SMALL, name="edges"
-    )(energy, flow)
+        edges_kernel, out_shape=edge_shapes, in_specs=[SMEM, VMEM, VMEM], out_specs=[VMEM] * 4, compiler_params=SMALL, name="edges"
+    )(odd, energy, flow)
     for iteration in range(STEPS):
         last = iteration == STEPS - 1
-        halos = send_edges(edges)
+        from_a, from_b, from_cols_b, from_cols_a = swap_edges(edges)
         outs = [float_of(channels, LANES), float_of(FIELDS, LANES)] + ([] if last else edge_shapes)
         energy, flow, *edges = pl.pallas_call(
             functools.partial(step_kernel, last),
             out_shape=outs,
-            in_specs=[SMEM] + [VMEM] * 10,
+            in_specs=[SMEM] * 2 + [VMEM] * 10,
             out_specs=[VMEM] * len(outs),
-            scratch_shapes=[pltpu.VMEM((channels + 8, LANES), jnp.float32), pltpu.VMEM((quads, LANES), jnp.bfloat16)],
+            scratch_shapes=[pltpu.VMEM((channels + 8, LANES), jnp.float32), pltpu.VMEM((quads, LANES), jnp.bfloat16)]
+            + [pltpu.VMEM(edge.shape, jnp.float32) for edge in edge_shapes],
             compiler_params=SMALL,
             name="last_step" if last else "step",
-        )(quad_index, energy, flow, wet, group_speed, coupling, stokes_kernel, *halos)
+        )(odd, quad_index, energy, flow, wet, group_speed, coupling, stokes_kernel, from_a, from_b, from_cols_a, from_cols_b)
     returned = exchange(energy, "comp")
+    half = groups // 2
+    far = lax.ppermute(flow, "grp", [(i, i ^ half) for i in range(groups)])
+    held = jnp.stack(ordered((group_place & half) != 0, flow, far))
+    held, returned = lax.optimization_barrier((held, returned))
+    tiles = [held] + [lax.ppermute(held, "grp", [(i, i ^ by) for i in range(groups)]) for by in range(1, half)]
     forecast = pl.pallas_call(
         from_points_kernel,
         out_shape=float_of(parts, rows_local, columns),
@@ -313,10 +321,13 @@
         compiler_params=SMALL,
         name="from_points",
     )(returned)
-    bits = groups.bit_length() - 1
-    tiles = gather_tiles(flow, groups, group_place).reshape((2,) * bits + (2, L, rows_local, cols_local))
-    order = (bits, bits + 1) + tuple(range(bits - 1, -1, -1)) + (bits + 2, bits + 3)
-    ocean = tiles.transpose(order).reshape(2, L, groups * rows_local, cols_local)
+    bit = 1
+    while bit < half:
+        upper = (group_place & bit) != 0
+        tiles = [jnp.where(upper, tiles[j ^ bit], tiles[j]) for j in range(half)]
+        bit *= 2
+    fields = jnp.stack(tiles).reshape(half, 2, 2, L, rows_local, cols_local)
+    ocean = fields.transpose(2, 3, 1, 0, 4, 5).reshape(2, L, groups * rows_local, cols_local)
     return forecast, ocean
 
 

time: 152 us -> 152 us (level)
  waiting for transfers between devices: 45.6 us -> 32.6 us
  starting transfers between devices: 54.8 us -> 65.6 us
    ppermute x11 -> x12, waiting for transfers between devices: 31.3 us -> 12.4 us  [the longest x1 10.6 us: local(): far = lax.ppermute(flow, 'grp', [(i, i ^ half) for i in range(groups)])]
    ppermute x11 -> x12, starting transfers between devices: 31.9 us -> 39.8 us  [the longest x8 27.4 us: swap(): lax.ppermute(value, axis, [(i, j) for i, j in enumerate(partner) if 0 <=...]
    all_to_all x2, waiting for transfers between devices: 14.2 us -> 20.3 us  [exchange(): moved = lax.all_to_all(lines, axis, split_axis=0, concat_axis=0, tiled=True)]
    all_to_all x2, starting transfers between devices: 23 us -> 25.9 us  [exchange(): moved = lax.all_to_all(lines, axis, split_axis=0, concat_axis=0, tiled=True)]
    reshape x2 -> x0, local copies, waits for them, and re-layouts: 2.65 us -> none  [local(): gather_tiles(flow, groups, group_place)]
    unnamed x21 -> x27, local copies, waits for them, and re-layouts: 5.17 us -> 6.61 us
  transfers between devices with their start and end apart: 13 -> 14, of which waited for: 8 -> 7; matrix products, arithmetic and copies ran while one was open for 6% -> 4% of each run, Pallas kernels for 0% -> 2%
where the time goes in v3:
time: 152 us; the launch traced here: 149 us
  starting transfers between devices  65.6 us (43%)
  Pallas kernels  36.8 us (24%)
  waiting for transfers between devices  32.6 us (21%)
  local copies, waits for them, and re-layouts  11.4 us (8%)
    pallas_call x2, Pallas kernels, local(): pl.pallas_call(functools.partial(step_kernel, last), out_shape=outs, in_s...  31.1 us
    ppermute x8, starting transfers between devices, swap(): lax.ppermute(value, axis, [(i, j) for i, j in enumerate(partner) if 0 <=...  27.4 us
    all_to_all x2, starting transfers between devices, exchange(): moved = lax.all_to_all(lines, axis, split_axis=0, concat_axis=0, tiled=True)  25.9 us
    all_to_all x2, waiting for transfers between devices, exchange(): moved = lax.all_to_all(lines, axis, split_axis=0, concat_axis=0, tiled=True)  20.3 us
    ppermute x1, waiting for transfers between devices, local(): far = lax.ppermute(flow, 'grp', [(i, i ^ half) for i in range(groups)])  10.6 us
    ppermute x3, starting transfers between devices, local(): lax.ppermute(held, 'grp', [(i, i ^ by) for i in range(groups)])  10.4 us
    unnamed x27, local copies, waits for them, and re-layouts  6.61 us
  transfers between devices with their start and end apart: 14, of which 7 were waited for; matrix products, arithmetic and copies ran while one was open for 4% of the time, Pallas kernels for 2%

profile of v3, /device:TPU:6, one launch (start us, length us, event | category | flops | bytes accessed | tf_op | source)
XLA Modules:
  0.0 148.9 jit_solution(12059572162629380092)
XLA Ops:
  0.6 0.0 copy-start
  0.6 0.0 copy-start.1
  0.7 0.0 copy-start.5
  0.7 1.2 copy-done.5
  1.9 1.6 %to_points.1 = f32[1152,128]{1,0:T(8,128)S(1)} custom-call(f32[18,8,1024]{2,1,0:T(8,128)S(1)} %copy-done.5), custom_call_target="tpu_custom_call" | custom-call | tf_op jit(solution)/shard_map/to_points/pallas_call | solution.py:289
  3.5 0.0 copy-start.2
  3.5 0.8 copy-done.2
  4.3 13.5 %all-to-all-start = ((f32[64,1,2304]{2,1,0:T(1,128)}), f32[64,1,2304]{2,1,0:T(1,128)S(1)}, u32[]{:S(2)}, u32[]{:S(2)}) async-start(f32[64,1,2304]{2,1,0:T(1,128)} %bitcast.17), calls=%async_computation | async-start | bytes 1179648 | tf_op jit(solution)/shard_map/all_to_all | solution.py:247
  17.8 0.8 fusion
  18.6 0.6 reshape.36.wet_ref
  19.2 0.0 copy-done
  19.2 0.8 constant_dynamic-slice_fusion
  20.1 1.7 %copy.18 = f32[2,16,8,16]{3,2,1,0:T(8,128)} copy(f32[2,16,8,16]{2,3,1,0:T(8,128)} %constant_dynamic-slice_fusion) | data formatting | bytes 32768 | tf_op jit(solution)/shard_map/dynamic_slice | solution.py:285
  21.8 1.0 reshape.37.f_ref.f_in_ref
  22.8 0.6 pad_add_fusion.odd_ref
  23.4 13.6 %all-to-all-done = f32[64,1,2304]{2,1,0:T(1,128)S(1)} async-done(((f32[64,1,2304]{2,1,0:T(1,128)}), f32[64,1,2304]{2,1,0:T(1,128)S(1)}, u32[]{:S(2)}, u32[]{:S(2)}) %all-to-all-start) | async-done | bytes 589856 | tf_op jit(solution)/shard_map/all_to_all | solution.py:247
  37.0 0.7 copy-done.10
  37.7 1.8 %edges.1 = (f32[152,128]{1,0:T(8,128)S(1)}, f32[152,128]{1,0:T(8,128)S(1)}, f32[80,128]{1,0:T(8,128)S(1)}, f32[80,128]{1,0:T(8,128)S(1)}) custom-call(s32[2]{0:T(128)S(1)} %copy-done.10, f32[1152,128]{1,0:T(8,128)S(1)} %bitcast.15, f32[32,128]{1,0:T(8,128)S(1)} %reshape.37.f_ref.f_in_ref), custom_call_target="tpu_custom_call" | custom-call | tf_op jit(solution)/shard_map/edges/pallas_call | solution.py:293
  39.5 2.7 %collective-permute-start = (f32[152,128]{1,0:T(8,128)S(1)}, f32[152,128]{1,0:T(8,128)S(1)}, u32[]{:S(2)}, u32[]{:S(2)}) collective-permute-start(f32[152,128]{1,0:T(8,128)S(1)} %get-tuple-element.24), channel_id=1, source_target_pairs={{0,1},{1,0},{2,3},{3,2},{4,5},{5,4},{6,7},{7,6},{8,9},{9,8},{10,11... | collective-permute-start | bytes 233480 | tf_op jit(solution)/shard_map/ppermute | solution.py:257
  42.2 8.8 %collective-permute-start.1 = (f32[152,128]{1,0:T(8,128)S(1)}, f32[152,128]{1,0:T(8,128)S(1)}, u32[]{:S(2)}, u32[]{:S(2)}) collective-permute-start(f32[152,128]{1,0:T(8,128)S(1)} %get-tuple-element.25), channel_id=1, source_target_pairs={{1,2},{2,1},{3,4},{4,3},{5,6},{6,5},{9,10},{10,9},{11,12},{12,11},... | collective-permute-start | bytes 233480 | tf_op jit(solution)/shard_map/ppermute | solution.py:257
  51.0 1.9 %collective-permute-start.2 = (f32[80,128]{1,0:T(8,128)S(1)}, f32[80,128]{1,0:T(8,128)S(1)}, u32[]{:S(2)}, u32[]{:S(2)}) collective-permute-start(f32[80,128]{1,0:T(8,128)S(1)} %get-tuple-element.26), channel_id=1, source_target_pairs={{0,8},{8,0},{16,24},{24,16},{32,40},{40,32},{48,56},{56,48},{64,72... | collective-permute-start | bytes 122888 | tf_op jit(solution)/shard_map/ppermute | solution.py:257
  52.9 0.7 collective-permute-start.3
  53.6 0.5 collective-permute-done.2.cols_a_ref
  54.1 0.0 collective-permute-done.3.cols_b_ref
  54.1 0.0 collective-permute-done.rows_a_ref
  54.1 0.4 collective-permute-done.1.rows_b_ref
  54.5 0.0 copy-done.1
  54.5 0.0 copy-done.6
  54.5 0.0 copy-done.7
  54.5 0.0 copy-start.3
  54.5 0.9 copy-done.3
  55.4 0.6 copy-done.8
  56.1 0.7 copy-done.11
  56.7 15.9 %step.1 = (f32[1152,128]{1,0:T(8,128)S(1)}, f32[32,128]{1,0:T(8,128)S(1)}, f32[152,128]{1,0:T(8,128)S(1)}, f32[152,128]{1,0:T(8,128)S(1)}, f32[80,128]{1,0:T(8,128)S(1)}, /*index=5*/f32[80,128]{1,0:T(8,128)S(1)}) custom-call(s32[2]{0:T(128)S(1)} %copy-done.11, s32[4,1152]{1,0:T(4,128)S(1)} %copy-done.6, f32[1152,128]{1,0:T(8,128)S(1)} %bitcast.16, ...), custom_call_target="tpu_custom_call" | custom-call | tf_op jit(solution)/shard_map/step/pallas_call | solution.py:300
  72.7 1.9 %collective-permute-start.4 = (f32[152,128]{1,0:T(8,128)S(1)}, f32[152,128]{1,0:T(8,128)S(1)}, u32[]{:S(2)}, u32[]{:S(2)}) collective-permute-start(f32[152,128]{1,0:T(8,128)S(1)} %get-tuple-element.30), channel_id=1, source_target_pairs={{0,1},{1,0},{2,3},{3,2},{4,5},{5,4},{6,7},{7,6},{8,9},{9,8},{10,11... | collective-permute-start | bytes 233480 | tf_op jit(solution)/shard_map/ppermute | solution.py:257
  74.6 8.8 %collective-permute-start.5 = (f32[152,128]{1,0:T(8,128)S(1)}, f32[152,128]{1,0:T(8,128)S(1)}, u32[]{:S(2)}, u32[]{:S(2)}) collective-permute-start(f32[152,128]{1,0:T(8,128)S(1)} %get-tuple-element.31), channel_id=1, source_target_pairs={{1,2},{2,1},{3,4},{4,3},{5,6},{6,5},{9,10},{10,9},{11,12},{12,11},... | collective-permute-start | bytes 233480 | tf_op jit(solution)/shard_map/ppermute | solution.py:257
  83.4 1.9 %collective-permute-start.6 = (f32[80,128]{1,0:T(8,128)S(1)}, f32[80,128]{1,0:T(8,128)S(1)}, u32[]{:S(2)}, u32[]{:S(2)}) collective-permute-start(f32[80,128]{1,0:T(8,128)S(1)} %get-tuple-element.32), channel_id=1, source_target_pairs={{0,8},{8,0},{16,24},{24,16},{32,40},{40,32},{48,56},{56,48},{64,72... | collective-permute-start | bytes 122888 | tf_op jit(solution)/shard_map/ppermute | solution.py:257
  85.3 0.7 collective-permute-start.7
  86.0 0.5 collective-permute-done.6.cols_a_ref
  86.5 0.0 collective-permute-done.7.cols_b_ref
  86.5 0.0 collective-permute-done.4.rows_a_ref
  86.5 0.4 collective-permute-done.5.rows_b_ref
  86.9 0.0 copy-done.4
  86.9 0.0 copy-done.12
  86.9 0.6 copy-done.9
  87.5 15.2 %last_step.1 = (f32[1152,128]{1,0:T(8,128)}, f32[32,128]{1,0:T(8,128)S(1)}) custom-call(s32[2]{0:T(128)S(1)} %copy-done.12, s32[4,1152]{1,0:T(4,128)S(1)} %copy-done.6, f32[1152,128]{1,0:T(8,128)S(1)} %get-tuple-element.28.e_in_ref, f32[32,128]{1,0:T(8,128)S(1)} %get-tuple-element.29.f_in_ref, f32[1,128]{1,0:T(1,128)S(1)} %copy-done.9, ...), custom_call_target="tpu_custom_call" | custom-call | tf_op jit(solution)/shard_map/last_step/pallas_call | solution.py:300
  102.7 12.4 %all-to-all-start.1 = ((f32[64,1,2304]{2,1,0:T(1,128)}), f32[64,1,2304]{2,1,0:T(1,128)S(1)}, u32[]{:S(2)}, u32[]{:S(2)}) async-start(f32[64,1,2304]{2,1,0:T(1,128)} %bitcast.6), calls=%async_computation.1 | async-start | bytes 1179648 | tf_op jit(solution)/shard_map/all_to_all | solution.py:247
  115.1 1.9 %collective-permute-start.8 = (f32[32,128]{1,0:T(8,128)S(1)}, f32[32,128]{1,0:T(8,128)S(1)}, u32[]{:S(2)}, u32[]{:S(2)}) collective-permute-start(f32[32,128]{1,0:T(8,128)S(1)} %get-tuple-element.34), channel_id=1, source_target_pairs={{0,4},{1,5},{2,6},{3,7},{4,0},{5,1},{6,2},{7,3},{8,12},{9,13},{10,... | collective-permute-start | bytes 49160 | tf_op jit(solution)/shard_map/ppermute | solution.py:312
  117.0 10.6 %collective-permute-done.8 = f32[32,128]{1,0:T(8,128)S(1)} collective-permute-done((f32[32,128]{1,0:T(8,128)S(1)}, f32[32,128]{1,0:T(8,128)S(1)}, u32[]{:S(2)}, u32[]{:S(2)}) %collective-permute-start.8) | collective-permute-done | bytes 16416 | tf_op jit(solution)/shard_map/ppermute | solution.py:312
  127.6 6.7 %all-to-all-done.1 = f32[64,1,2304]{2,1,0:T(1,128)S(1)} async-done(((f32[64,1,2304]{2,1,0:T(1,128)}), f32[64,1,2304]{2,1,0:T(1,128)S(1)}, u32[]{:S(2)}, u32[]{:S(2)}) %all-to-all-start.1) | async-done | bytes 589856 | tf_op jit(solution)/shard_map/all_to_all | solution.py:247
  134.3 1.9 %collective-permute-start.11 = (f32[2,32,128]{2,1,0:T(8,128)S(1)}, f32[2,32,128]{2,1,0:T(8,128)S(1)}, u32[]{:S(2)}, u32[]{:S(2)}) collective-permute-start(f32[2,32,128]{2,1,0:T(8,128)S(1)} %pad_maximum_fusion.1), channel_id=1, source_target_pairs={{0,1},{1,0},{2,3},{3,2},{4,5},{5,4},{6,7},{7,6},{8,9},{9,8},{10,11... | collective-permute-start | bytes 98312 | tf_op jit(solution)/shard_map/ppermute | solution.py:315
  136.2 3.3 %collective-permute-start.10 = (f32[2,32,128]{2,1,0:T(8,128)S(1)}, f32[2,32,128]{2,1,0:T(8,128)S(1)}, u32[]{:S(2)}, u32[]{:S(2)}) collective-permute-start(f32[2,32,128]{2,1,0:T(8,128)S(1)} %pad_maximum_fusion.1), channel_id=1, source_target_pairs={{0,2},{1,3},{2,0},{3,1},{4,6},{5,7},{6,4},{7,5},{8,10},{9,11},{10,... | collective-permute-start | bytes 98312 | tf_op jit(solution)/shard_map/ppermute | solution.py:315
  139.5 5.2 %collective-permute-start.9 = (f32[2,32,128]{2,1,0:T(8,128)S(1)}, f32[2,32,128]{2,1,0:T(8,128)S(1)}, u32[]{:S(2)}, u32[]{:S(2)}) collective-permute-start(f32[2,32,128]{2,1,0:T(8,128)S(1)} %pad_maximum_fusion.1), channel_id=1, source_target_pairs={{0,3},{1,2},{2,1},{3,0},{4,7},{5,6},{6,5},{7,4},{8,11},{9,10},{10,... | collective-permute-start | bytes 98312 | tf_op jit(solution)/shard_map/ppermute | solution.py:315
  144.7 2.4 %from_points.1 = f32[18,8,1024]{2,1,0:T(8,128)} custom-call(f32[1152,128]{1,0:T(8,128)S(1)} %bitcast.18), custom_call_target="tpu_custom_call" | custom-call | tf_op jit(solution)/shard_map/from_points/pallas_call | solution.py:316
  147.1 0.0 collective-permute-done.11
  147.1 0.0 collective-permute-done.10
  147.1 0.0 collective-permute-done.9
  147.1 0.1 stack.39
  147.3 0.1 stack.40
  147.4 0.1 stack.41
  147.5 0.1 stack.42
  147.7 0.1 pad_maximum_fusion
  147.8 0.1 copy.25
  147.9 1.0 copy.24
  (11 shorter events, 0.0 us)
Async XLA Ops:
  0.6 18.6 %copy-start = (f32[2,16,64,16]{2,3,1,0:T(8,128)S(1)}, f32[2,16,64,16]{2,3,1,0:T(8,128)}, u32[]{:S(2)}) copy-start(f32[2,16,64,16]{2,3,1,0:T(8,128)} %param.13) | copy-start | bytes 393220
  0.6 53.9 %copy-start.1 = (bf16[1152,1152]{1,0:T(8,128)(2,1)S(1)}, bf16[1152,1152]{1,0:T(8,128)(2,1)}, u32[]{:S(2)}) copy-start(bf16[1152,1152]{1,0:T(8,128)(2,1)} %coupling_ref.3) | copy-start | bytes 7962628
  0.7 1.2 copy-start.5
  1.9 52.7 %copy-start.6 = (s32[4,1152]{1,0:T(4,128)S(1)}, s32[4,1152]{1,0:T(4,128)}, u32[]{:S(2)}) copy-start(s32[4,1152]{1,0:T(4,128)} %index_ref.3) | copy-start | bytes 55300
  1.9 52.7 %copy-start.7 = (f32[2,1152]{1,0:T(2,128)S(1)}, f32[2,1152]{1,0:T(2,128)}, u32[]{:S(2)}) copy-start(f32[2,1152]{1,0:T(2,128)} %speed_ref.3) | copy-start | bytes 27652
  3.5 0.8 copy-start.2
  4.3 32.7 %all-to-all-start = ((f32[64,1,2304]{2,1,0:T(1,128)}), f32[64,1,2304]{2,1,0:T(1,128)S(1)}, u32[]{:S(2)}, u32[]{:S(2)}) async-start(f32[64,1,2304]{2,1,0:T(1,128)} %bitcast.17), calls=%async_computation | async-start | bytes 1179648 | tf_op jit(solution)/shard_map/all_to_all | solution.py:247
  37.0 49.9 %copy-start.4 = (f32[32,1152]{1,0:T(8,128)S(1)}, f32[32,1152]{1,0:T(8,128)}, u32[]{:S(2)}) copy-start(f32[32,1152]{1,0:T(8,128)} %profile_ref.3) | copy-start | bytes 442372
  37.0 0.7 copy-start.10
  37.7 49.2 %copy-start.12 = (s32[2]{0:T(128)S(1)}, s32[2]{0:T(128)}, u32[]{:S(2)}) copy-start(s32[2]{0:T(128)} %pad_add_fusion.odd_ref) | copy-start | bytes 28
  39.5 14.7 %collective-permute-start = (f32[152,128]{1,0:T(8,128)S(1)}, f32[152,128]{1,0:T(8,128)S(1)}, u32[]{:S(2)}, u32[]{:S(2)}) collective-permute-start(f32[152,128]{1,0:T(8,128)S(1)} %get-tuple-element.24), channel_id=1, source_target_pairs={{0,1},{1,0},{2,3},{3,2},{4,5},{5,4},{6,7},{7,6},{8,9},{9,8},{10,11... | collective-permute-start | bytes 233480 | tf_op jit(solution)/shard_map/ppermute | solution.py:257
  42.2 12.3 %collective-permute-start.1 = (f32[152,128]{1,0:T(8,128)S(1)}, f32[152,128]{1,0:T(8,128)S(1)}, u32[]{:S(2)}, u32[]{:S(2)}) collective-permute-start(f32[152,128]{1,0:T(8,128)S(1)} %get-tuple-element.25), channel_id=1, source_target_pairs={{1,2},{2,1},{3,4},{4,3},{5,6},{6,5},{9,10},{10,9},{11,12},{12,11},... | collective-permute-start | bytes 233480 | tf_op jit(solution)/shard_map/ppermute | solution.py:257
  51.0 3.1 %collective-permute-start.2 = (f32[80,128]{1,0:T(8,128)S(1)}, f32[80,128]{1,0:T(8,128)S(1)}, u32[]{:S(2)}, u32[]{:S(2)}) collective-permute-start(f32[80,128]{1,0:T(8,128)S(1)} %get-tuple-element.26), channel_id=1, source_target_pairs={{0,8},{8,0},{16,24},{24,16},{32,40},{40,32},{48,56},{56,48},{64,72... | collective-permute-start | bytes 122888 | tf_op jit(solution)/shard_map/ppermute | solution.py:257
  52.9 1.2 collective-permute-start.3
  54.5 0.9 copy-start.3
  55.4 0.6 copy-start.8
  56.1 0.7 copy-start.11
  72.7 13.9 %collective-permute-start.4 = (f32[152,128]{1,0:T(8,128)S(1)}, f32[152,128]{1,0:T(8,128)S(1)}, u32[]{:S(2)}, u32[]{:S(2)}) collective-permute-start(f32[152,128]{1,0:T(8,128)S(1)} %get-tuple-element.30), channel_id=1, source_target_pairs={{0,1},{1,0},{2,3},{3,2},{4,5},{5,4},{6,7},{7,6},{8,9},{9,8},{10,11... | collective-permute-start | bytes 233480 | tf_op jit(solution)/shard_map/ppermute | solution.py:257
  74.6 12.3 %collective-permute-start.5 = (f32[152,128]{1,0:T(8,128)S(1)}, f32[152,128]{1,0:T(8,128)S(1)}, u32[]{:S(2)}, u32[]{:S(2)}) collective-permute-start(f32[152,128]{1,0:T(8,128)S(1)} %get-tuple-element.31), channel_id=1, source_target_pairs={{1,2},{2,1},{3,4},{4,3},{5,6},{6,5},{9,10},{10,9},{11,12},{12,11},... | collective-permute-start | bytes 233480 | tf_op jit(solution)/shard_map/ppermute | solution.py:257
  83.4 3.1 %collective-permute-start.6 = (f32[80,128]{1,0:T(8,128)S(1)}, f32[80,128]{1,0:T(8,128)S(1)}, u32[]{:S(2)}, u32[]{:S(2)}) collective-permute-start(f32[80,128]{1,0:T(8,128)S(1)} %get-tuple-element.32), channel_id=1, source_target_pairs={{0,8},{8,0},{16,24},{24,16},{32,40},{40,32},{48,56},{56,48},{64,72... | collective-permute-start | bytes 122888 | tf_op jit(solution)/shard_map/ppermute | solution.py:257
  85.3 1.2 collective-permute-start.7
  86.9 0.6 copy-start.9
  102.7 31.5 %all-to-all-start.1 = ((f32[64,1,2304]{2,1,0:T(1,128)}), f32[64,1,2304]{2,1,0:T(1,128)S(1)}, u32[]{:S(2)}, u32[]{:S(2)}) async-start(f32[64,1,2304]{2,1,0:T(1,128)} %bitcast.6), calls=%async_computation.1 | async-start | bytes 1179648 | tf_op jit(solution)/shard_map/all_to_all | solution.py:247
  115.1 12.5 %collective-permute-start.8 = (f32[32,128]{1,0:T(8,128)S(1)}, f32[32,128]{1,0:T(8,128)S(1)}, u32[]{:S(2)}, u32[]{:S(2)}) collective-permute-start(f32[32,128]{1,0:T(8,128)S(1)} %get-tuple-element.34), channel_id=1, source_target_pairs={{0,4},{1,5},{2,6},{3,7},{4,0},{5,1},{6,2},{7,3},{8,12},{9,13},{10,... | collective-permute-start | bytes 49160 | tf_op jit(solution)/shard_map/ppermute | solution.py:312
  134.3 12.8 %collective-permute-start.11 = (f32[2,32,128]{2,1,0:T(8,128)S(1)}, f32[2,32,128]{2,1,0:T(8,128)S(1)}, u32[]{:S(2)}, u32[]{:S(2)}) collective-permute-start(f32[2,32,128]{2,1,0:T(8,128)S(1)} %pad_maximum_fusion.1), channel_id=1, source_target_pairs={{0,1},{1,0},{2,3},{3,2},{4,5},{5,4},{6,7},{7,6},{8,9},{9,8},{10,11... | collective-permute-start | bytes 98312 | tf_op jit(solution)/shard_map/ppermute | solution.py:315
  136.2 10.9 %collective-permute-start.10 = (f32[2,32,128]{2,1,0:T(8,128)S(1)}, f32[2,32,128]{2,1,0:T(8,128)S(1)}, u32[]{:S(2)}, u32[]{:S(2)}) collective-permute-start(f32[2,32,128]{2,1,0:T(8,128)S(1)} %pad_maximum_fusion.1), channel_id=1, source_target_pairs={{0,2},{1,3},{2,0},{3,1},{4,6},{5,7},{6,4},{7,5},{8,10},{9,11},{10,... | collective-permute-start | bytes 98312 | tf_op jit(solution)/shard_map/ppermute | solution.py:315
  139.5 7.6 %collective-permute-start.9 = (f32[2,32,128]{2,1,0:T(8,128)S(1)}, f32[2,32,128]{2,1,0:T(8,128)S(1)}, u32[]{:S(2)}, u32[]{:S(2)}) collective-permute-start(f32[2,32,128]{2,1,0:T(8,128)S(1)} %pad_maximum_fusion.1), channel_id=1, source_target_pairs={{0,3},{1,2},{2,1},{3,0},{4,7},{5,6},{6,5},{7,4},{8,11},{9,10},{10,... | collective-permute-start | bytes 98312 | tf_op jit(solution)/shard_map/ppermute | solution.py:315
